TPU v7x, 32 devices: a whole 2x2x4 slice. The times are simulated.
32 devices in a mesh: grp: 4 (over y, x), body: 8 (over z, core).
Axes of the slice: x: 2, y: 2, z: 4, core: 2. Of those that a mesh axis runs over, the one named last changes fastest.
Arguments:
- incident: bfloat16 [32, 16, 512], P(('grp', 'body')), may hold values from -6 to 6
- exciting: float32 [32, 16, 512], P(('grp', 'body')), may hold values from -6 to 6
- t_matrices: bfloat16 [32, 2, 256, 256], P(('grp', 'body')), may hold values from -0.1875 to 0.1875
- hankel_rows: bfloat16 [225, 2, 512], replicated, may hold values from -0.09375 to 0.09375
- offsets: int32 [32, 8], P(('grp', 'body')), may hold values from 0 to 224
- lattice_slots: int32 [32], P('grp'), may hold values from 0 to 7, as said below
- up_maps: bfloat16 [32, 2, 256, 512], P(('grp', 'body')), may hold values from -0.125 to 0.125
- down_maps: bfloat16 [32, 2, 512, 256], P(('grp', 'body')), may hold values from -0.1875 to 0.1875
- group_maps: bfloat16 [4, 4, 2, 512, 512], P('grp', None, None, 'body'), may hold values from -0.09375 to 0.09375
Outputs:
- updated: float32 [32, 16, 512], P(('grp', 'body'))
Inputs may be any that keep to these rules, and one draw needn't show every extreme that they name: `lattice_slots`: within each group the 8 columns stand at the slots 0 to 7, one column a slot.
All inputs are finite; a program needn't handle non-finite values.
Results may differ from a plain program's by a relative error of at most 0.0034.
Values may be sent and summed in bfloat16 or wider, within the bound.
No kernel may reach another device: no remote copies, remote signals or barrier semaphores. Data moves between devices by JAX's collectives and lax.ppermute only.
A program may use at most 64 MiB of HBM per device.

v0:
```python
import math

import jax
import jax.numpy as jnp
from jax import lax
from jax.sharding import PartitionSpec as P


def complex_apply(form, values, real_mats, imag_mats):
    half_width = values.shape[-1] // 2
    real_values = values[..., :half_width]
    imag_values = values[..., half_width:]
    real_out = jnp.einsum(
        form, real_values, real_mats, preferred_element_type=jnp.float32
    ) - jnp.einsum(form, imag_values, imag_mats, preferred_element_type=jnp.float32)
    imag_out = jnp.einsum(
        form, real_values, imag_mats, preferred_element_type=jnp.float32
    ) + jnp.einsum(form, imag_values, real_mats, preferred_element_type=jnp.float32)
    return jnp.concatenate([real_out, imag_out], axis=-1)


def toeplitz_mats(sequences):
    length = sequences.shape[-1] // 2
    repeats = (1,) * (sequences.ndim - 1) + (length,)
    tiled = jnp.tile(sequences, repeats)
    window = tiled[..., length : length + length * (2 * length - 1)]
    return window.reshape(sequences.shape[:-1] + (length, 2 * length - 1))[..., :length]


def local(
    incident,
    exciting,
    t_matrices,
    hankel_rows,
    offsets,
    lattice_slots,
    up_maps,
    down_maps,
    group_maps,
):
    body_index = lax.axis_index("body")
    group_index = lax.axis_index("grp")
    local_count = incident.shape[0]
    scattered = complex_apply("iln,inm->ilm", incident, t_matrices[:, 0], t_matrices[:, 1]).astype(
        jnp.bfloat16
    )
    own_members = body_index * local_count + jnp.arange(local_count, dtype=jnp.int32)
    zero_seq = jnp.zeros((), jnp.bfloat16)
    empty = jnp.zeros(scattered.shape, jnp.float32)
    total = empty
    piece = lax.all_gather(scattered, "body", axis=0, tiled=True)
    width = piece.shape[0]
    block_rows = math.gcd(width, 4)
    table_rows = jnp.take(offsets, lattice_slots, axis=1)
    sequences = jnp.take(hankel_rows, table_rows, axis=0)
    sources = jnp.arange(width, dtype=jnp.int32)
    keep = own_members[:, None] != sources[None, :]
    sequences = jnp.where(keep[:, :, None, None], sequences, zero_seq)
    sequences = sequences.reshape(
        (local_count, width // block_rows, block_rows) + sequences.shape[2:]
    ).swapaxes(0, 1)
    pieces = piece.reshape((width // block_rows, block_rows) + piece.shape[1:])

    def one_block(accum, inputs):
        block_seqs, block_piece = inputs
        mats = toeplitz_mats(block_seqs)
        return (
            accum + complex_apply("jln,tjnm->tlm", block_piece, mats[:, :, 0], mats[:, :, 1]),
            None,
        )

    total, _ = lax.scan(one_block, total, (sequences, pieces))
    partial_value = complex_apply("iln,inq->lq", scattered, up_maps[:, 0], up_maps[:, 1])
    expansion = lax.psum(partial_value, "body").astype(jnp.bfloat16)
    block_width = group_maps.shape[3]
    full_width = group_maps.shape[4]
    real_block = lax.dynamic_slice_in_dim(expansion, body_index * block_width, block_width, 1)
    imag_block = lax.dynamic_slice_in_dim(
        expansion, full_width + body_index * block_width, block_width, 1
    )
    own_block = jnp.concatenate([real_block, imag_block], axis=-1)[None]
    piece = lax.all_gather(own_block, "grp", axis=0, tiled=True)
    width = piece.shape[0]
    sources = jnp.arange(width, dtype=jnp.int32)
    piece = jnp.where((sources != group_index)[:, None, None], piece, zero_seq)
    mats = group_maps[0]
    incoming_part = complex_apply("hln,hnq->lq", piece, mats[:, 0], mats[:, 1])
    incoming = lax.psum(incoming_part, "body").astype(jnp.bfloat16)
    far = complex_apply("lq,iqp->ilp", incoming, down_maps[:, 0], down_maps[:, 1])
    return exciting + total + far


def solution(mesh):
    return jax.shard_map(
        local,
        mesh=mesh,
        in_specs=(
            P(("grp", "body"), None, None),
            P(("grp", "body"), None, None),
            P(("grp", "body"), None, None, None),
            P(),
            P(("grp", "body"), None),
            P("grp"),
            P(("grp", "body"), None, None, None),
            P(("grp", "body"), None, None, None),
            P("grp", None, None, "body", None),
        ),
        out_specs=P(("grp", "body"), None, None),
        check_vma=False,
    )
```

profile of v0, /device:TPU:0, one launch (start us, length us, event | category | flops | bytes accessed | tf_op | source)
XLA Modules:
  0.0 120.4 jit_solution(14881951126355513148)
XLA Ops:
  0.0 1.1 fusion.38
  1.1 1.1 fusion.12
  2.2 1.1 fusion.20
  3.3 1.1 fusion.34
  4.5 1.1 fusion.13
  5.5 1.1 convolution_add_fusion
  6.6 1.1 fusion.24
  7.7 1.1 convolution_subtract_fusion
  8.8 0.0 copy-start.5
  8.9 0.0 copy-start.1
  8.9 30.7 %psum.14 = bf16[16,1024]{1,0:T(8,128)(2,1)S(1)} all-reduce(f32[16,1024]{1,0:T(8,128)S(1)} %pad_maximum_fusion), channel_id=1, replica_groups=mesh['grp'=4,'body'=8] {'body'}, use_global_device_ids=true, to_apply=%region_2.3 | all-reduce | flops 16384 | bytes 98304 | tf_op jit(solution)/shard_map/psum | solution.py:74
  39.6 0.1 constant_dynamic-slice_fusion.1
  39.7 0.1 pad_maximum_fusion.3
  39.8 8.2 %all-gather = bf16[64,128]{1,0:T(8,128)(2,1)S(1)} all-gather(bf16[16,128]{1,0:T(8,128)(2,1)S(1)} %pad_maximum_fusion.3), channel_id=2, replica_groups=mesh['grp'=4,'body'=8] {'grp'}, dimensions={0}, use_global_device_ids=true | all-gather | bytes 20480 | tf_op jit(solution)/shard_map/all_gather | solution.py:82
  48.0 0.1 broadcast_select_fusion.2
  48.1 0.2 convolution_bitcast_fusion.7
  48.3 0.3 fusion.9
  48.5 0.2 convolution_bitcast_fusion.5
  48.7 0.3 fusion.8
  49.0 26.3 %psum.15 = bf16[16,1024]{1,0:T(8,128)(2,1)S(1)} all-reduce(f32[16,1024]{1,0:T(8,128)S(1)} %pad_maximum_fusion.1), channel_id=1, replica_groups=mesh['grp'=4,'body'=8] {'body'}, use_global_device_ids=true, to_apply=%region_3.4 | all-reduce | flops 16384 | bytes 98304 | tf_op jit(solution)/shard_map/psum | solution.py:88
  75.3 0.1 fusion.18
  75.5 0.2 fusion.11
  75.6 0.2 fusion.14
  75.8 0.2 fusion.10
  75.9 14.0 %all_gather.6 = bf16[8,16,512]{2,1,0:T(8,128)(2,1)S(1)} all-gather(bf16[1,16,512]{2,1,0:T(8,128)(2,1)S(1)} %pad_maximum_fusion.2), channel_id=1, replica_groups=mesh['grp'=4,'body'=8] {'body'}, dimensions={0}, use_global_device_ids=true | all-gather | bytes 147456 | tf_op jit(solution)/shard_map/all_gather | solution.py:51
  89.9 0.6 gather_fusion
  90.6 0.6 gather_fusion.1
  91.2 0.1 broadcast_in_dim.54
  91.3 0.1 fusion.44
  91.4 0.0 copy-start.4
  91.4 28.3 %while.11 = (s32[]{:T(128)}, f32[1,16,512]{2,1,0:T(8,128)S(1)}, bf16[2,1,4,2,512]{4,3,2,1,0:T(2,128)(2,1)S(1)}, bf16[2,4,16,512]{3,2,1,0:T(8,128)(2,1)S(1)}, s32[]{:T(128)}, /*index=5*/s32[]{:T(128)}) while((s32[]{:T(128)}, f32[1,16,512]{2,1,0:T(8,128)S(1)}, bf16[2,1,4,2,512]{4,3,2,1,0:T(2,128)(2,1)S(1)}, ...), condition=%wide.region_1.2_spmd.clone, body=%wide.region_0.1_spmd.clone.sunk | while | flops 33587200 | bytes 17244244 | solution.py:72
  91.5 0.2 tile.16
  91.6 2.8 %tile.17 = bf16[1,4,2,131072]{3,2,1,0:T(2,128)(2,1)} reshape(bf16[4,2,256,512]{3,2,1,0:T(8,128)(2,1)S(1)} %tile.16) | data formatting | bytes 4194304 | tf_op jit(solution)/shard_map/while/body/eval_jaxpr/tile | solution.py:25
  94.4 4.3 %slice.213 = bf16[1,4,2,130816]{3,2,1,0:T(2,128)(2,1)} slice(bf16[1,4,2,131072]{3,2,1,0:T(2,128)(2,1)} %tile.17), slice={[0:1], [0:4], [0:2], [256:131072]} | slice | bytes 4186112 | tf_op jit(solution)/shard_map/while/body/eval_jaxpr/slice | solution.py:26
  98.7 6.1 %reshape.255 = bf16[1,4,2,256,511]{4,3,2,1,0:T(8,128)(2,1)S(1)} reshape(bf16[1,4,2,130816]{3,2,1,0:T(2,128)(2,1)} %slice.213) | data formatting | bytes 4186112 | tf_op jit(solution)/shard_map/while/body/eval_jaxpr/reshape | solution.py:27
  104.8 0.2 convolution_bitcast_fusion.11
  105.0 0.2 fusion.76
  105.2 0.2 convolution_bitcast_fusion.10
  105.4 0.2 fusion.75
  105.6 0.2 tile.16
  105.8 2.8 %tile.17 = bf16[1,4,2,131072]{3,2,1,0:T(2,128)(2,1)} reshape(bf16[4,2,256,512]{3,2,1,0:T(8,128)(2,1)S(1)} %tile.16) | data formatting | bytes 4194304 | tf_op jit(solution)/shard_map/while/body/eval_jaxpr/tile | solution.py:25
  108.5 4.3 %slice.213 = bf16[1,4,2,130816]{3,2,1,0:T(2,128)(2,1)} slice(bf16[1,4,2,131072]{3,2,1,0:T(2,128)(2,1)} %tile.17), slice={[0:1], [0:4], [0:2], [256:131072]} | slice | bytes 4186112 | tf_op jit(solution)/shard_map/while/body/eval_jaxpr/slice | solution.py:26
  112.9 6.1 %reshape.255 = bf16[1,4,2,256,511]{4,3,2,1,0:T(8,128)(2,1)S(1)} reshape(bf16[1,4,2,130816]{3,2,1,0:T(2,128)(2,1)} %slice.213) | data formatting | bytes 4186112 | tf_op jit(solution)/shard_map/while/body/eval_jaxpr/reshape | solution.py:27
  119.0 0.2 convolution_bitcast_fusion.11
  119.2 0.2 fusion.76
  119.4 0.2 convolution_bitcast_fusion.10
  119.6 0.2 fusion.75
  119.8 0.6 maximum_add_fusion.1
  (26 shorter events, 0.2 us)
Async XLA Ops:
  0.0 90.6 %copy-start = (bf16[225,2,512]{2,1,0:T(2,128)(2,1)S(1)}, bf16[225,2,512]{2,1,0:T(2,128)(2,1)}, u32[]{:S(2)}) copy-start(bf16[225,2,512]{2,1,0:T(2,128)(2,1)} %param.14) | copy-start | bytes 1382404
  0.0 48.0 %copy-start.3 = (bf16[1,4,2,64,512]{4,3,2,1,0:T(8,128)(2,1)S(1)}, bf16[1,4,2,64,512]{4,3,2,1,0:T(8,128)(2,1)}, u32[]{:S(2)}) copy-start(bf16[1,4,2,64,512]{4,3,2,1,0:T(8,128)(2,1)} %param.19) | copy-start | bytes 1572868
  3.3 72.0 %copy-start.2 = (bf16[1,2,512,256]{3,2,1,0:T(8,128)(2,1)S(1)}, bf16[1,2,512,256]{3,2,1,0:T(8,128)(2,1)}, u32[]{:S(2)}) copy-start(bf16[1,2,512,256]{3,2,1,0:T(8,128)(2,1)} %param.18) | copy-start | bytes 1572868
  8.8 81.1 %copy-start.5 = (s32[8]{0:T(128)S(1)}, s32[8]{0:T(128)}, u32[]{:S(2)}) copy-start(s32[8]{0:T(128)} %param.16) | copy-start | bytes 100
  8.9 81.1 %copy-start.1 = (s32[1,8]{1,0:T(1,128)S(1)}, s32[1,8]{1,0:T(1,128)}, u32[]{:S(2)}) copy-start(s32[1,8]{1,0:T(1,128)} %param.15) | copy-start | bytes 100
  91.4 28.4 %copy-start.4 = (f32[1,16,512]{2,1,0:T(8,128)S(1)}, f32[1,16,512]{2,1,0:T(8,128)}, u32[]{:S(2)}) copy-start(f32[1,16,512]{2,1,0:T(8,128)} %param.12) | copy-start | bytes 98308
where the time goes:
time: 121 us; the launch traced here: 120 us
  blocking collectives  79.2 us (65%)
  local copies, waits for them, and re-layouts  28.2 us (23%)
  matrix products  11.8 us (10%)
    psum x1, blocking collectives, local(): expansion = lax.psum(partial_value, 'body').astype(jnp.bfloat16)  30.7 us
    psum x1, blocking collectives, local(): incoming = lax.psum(incoming_part, 'body').astype(jnp.bfloat16)  26.3 us
    all_gather x1, blocking collectives, local(): piece = lax.all_gather(scattered, 'body', axis=0, tiled=True)  14 us
    reshape x2, local copies, waits for them, and re-layouts, toeplitz_mats(): window.reshape(sequences.shape[:-1] + (length, 2 * length - 1))  12.2 us
    slice x2, local copies, waits for them, and re-layouts, toeplitz_mats(): window = tiled[..., length:length + length * (2 * length - 1)]  8.67 us
    all_gather x1, blocking collectives, local(): piece = lax.all_gather(own_block, 'grp', axis=0, tiled=True)  8.18 us
    another operation x6, local copies, waits for them, and re-layouts, toeplitz_mats(): tiled = jnp.tile(sequences, repeats)  5.85 us
    dot_general x6, matrix products, complex_apply(): jnp.einsum(form, imag_values, real_mats, preferred_element_type=jnp.float32)  2.97 us

commit v1 on v0

v1 whole, which is shorter than its diff:
```python
import functools

import jax
import jax.numpy as jnp
from jax import lax
from jax.experimental import pallas as pl
from jax.experimental.pallas import tpu as pltpu
from jax.sharding import PartitionSpec as P

AXES = ("grp", "body")
SMEM = pl.BlockSpec(memory_space=pltpu.SMEM)
VMEM = pl.BlockSpec(memory_space=pltpu.VMEM)


def crossed(values):
    rows = values.shape[0] // 2
    real, imag = values[:rows], values[rows:]
    return jnp.concatenate(
        [jnp.concatenate([real, -imag], axis=1), jnp.concatenate([imag, real], axis=1)], axis=0
    )


def dot(left, right):
    return jnp.dot(left, right, preferred_element_type=jnp.float32)


def first_kernel(core, incident, offsets, t_mats, up, scattered, partial_sum, message):
    rows, modes = incident.shape[0], t_mats.shape[2]
    values = jnp.concatenate([incident[:, :modes], incident[:, modes:]], axis=0)
    own = dot(crossed(values), t_mats[...].reshape(2 * modes, modes)).astype(jnp.bfloat16)
    scattered[...] = own
    term = dot(crossed(own), up[...].reshape(2 * modes, up.shape[2]))
    partial_sum[...] = term

    @pl.when(core[0] == 0)
    def _():
        message[...] = term

    @pl.when(core[0] != 0)
    def _():
        message[:, :modes] = own.astype(jnp.float32)
        message[:, modes:] = jnp.zeros((2 * rows, message.shape[1] - modes), jnp.float32)
        message[0:1, modes : modes + offsets.shape[1]] = offsets[...].astype(jnp.float32)


def near_kernel(where, offsets, slots, table, pieces, near):
    chips, _, rows, modes = pieces.shape
    half = modes // 2

    @pl.when(where[0] == 0)
    def _():
        chip = where[1]
        for column in range(2):
            total = jnp.zeros((rows, 2 * modes), jnp.float32)
            for other in range(chips):
                for member in range(2):
                    source = (chip ^ other) * 2 + member
                    row = offsets[column, slots[source]]
                    sequence = table[row].astype(jnp.float32)
                    if other == 0 and member == column:
                        continue
                    mats = []
                    for part in range(2):
                        band = jnp.broadcast_to(sequence[part : part + 1], (half, 2 * modes))
                        band = pltpu.roll(band, 0, 1, stride=1, stride_axis=0)
                        band = band.astype(jnp.bfloat16)
                        mats.append(
                            jnp.concatenate(
                                [band[:, modes:], band[:, half : half + modes]], axis=0
                            )
                        )
                    total += dot(pieces[other, member], jnp.concatenate(mats, axis=1))
            top, low = total[: rows // 2], total[rows // 2 :]
            near[column, : rows // 2, :] = top[:, :modes] - low[:, modes:]
            near[column, rows // 2 :, :] = top[:, modes:] + low[:, :modes]


def group_kernel(where, pieces, own_maps, other_maps, incoming):
    groups, rows, width = pieces.shape
    total = jnp.zeros(incoming.shape, jnp.float32)
    for other in range(1, groups):
        source = where[0] ^ other
        mats = jnp.concatenate(
            [other_maps[source, 0], own_maps[source, 0], other_maps[source, 1], own_maps[source, 1]],
            axis=0,
        )
        total += dot(crossed(pieces[other]), mats)
    incoming[...] = total


def last_kernel(incoming, near, down, exciting, updated):
    modes = down.shape[2]
    rows = exciting.shape[0]
    far = dot(crossed(incoming[...]), down[...].reshape(2 * down.shape[1], modes)) + near[...]
    updated[:, :modes] = exciting[:, :modes] + far[:rows]
    updated[:, modes:] = exciting[:, modes:] + far[rows:]


def digits(count):
    found, shift = [], 0
    while (1 << shift) < count:
        found.append([k << shift for k in range(1, min(4, count >> shift))])
        shift += 2
    return found


def local(
    groups,
    bodies,
    incident,
    exciting,
    t_matrices,
    hankel_rows,
    offsets,
    lattice_slots,
    up_maps,
    down_maps,
    group_maps,
):
    body = lax.axis_index("body")
    group = lax.axis_index("grp")
    core, chip = body % 2, body // 2
    chips = bodies // 2
    rows, modes = incident.shape[1], t_matrices.shape[2]
    coefs = up_maps.shape[3]
    bf16, f32 = jnp.bfloat16, jnp.float32

    def exchange(values, even, odd):
        pairs = [(i, i ^ (odd if i % 2 else even)) for i in range(groups * bodies)]
        return lax.ppermute(values, AXES, pairs)

    def shaped(shape, dtype):
        return jax.ShapeDtypeStruct(shape, dtype)

    core_arg = core.astype(jnp.int32).reshape(1)
    other_maps = exchange(group_maps[0], 1, 1)
    scattered, partial_sum, message = pl.pallas_call(
        first_kernel,
        out_shape=(
            shaped((2 * rows, modes), bf16),
            shaped((2 * rows, coefs), f32),
            shaped((2 * rows, coefs), f32),
        ),
        in_specs=[SMEM] + [VMEM] * 4,
        out_specs=(VMEM,) * 3,
        name="first",
    )(core_arg, incident[0], offsets, t_matrices[0], up_maps[0])
    received = exchange(message, 1, 1)

    expansion = partial_sum + received
    pieces = jnp.stack([scattered, received[:, :modes].astype(bf16)])[None]
    both_offsets = jnp.concatenate(
        [offsets, received[0:1, modes : modes + offsets.shape[1]].astype(jnp.int32)], axis=0
    )
    for steps in digits(chips):
        sums = jnp.stack([expansion[:, :modes], expansion[:, modes:]]).astype(bf16)[None]
        sums = jnp.pad(sums, ((0, pieces.shape[0] - 1), (0, 0), (0, 0), (0, 0)))
        message = jnp.where(core == 1, sums, pieces)
        arrived = [exchange(message, 2 * step, 2 * step) for step in steps]
        for piece in arrived:
            expansion += jnp.concatenate([piece[0, 0], piece[0, 1]], axis=1).astype(f32)
        pieces = jnp.concatenate([pieces] + arrived, axis=0)
    block = coefs // chips
    own_block = lax.dynamic_slice_in_dim(expansion, chip * block, block, 1).astype(bf16)[None]

    near = pl.pallas_call(
        near_kernel,
        out_shape=shaped((2, 2 * rows, modes), f32),
        in_specs=[SMEM] * 3 + [VMEM] * 2,
        out_specs=VMEM,
        name="near",
    )(jnp.stack([core, chip]).astype(jnp.int32), both_offsets, lattice_slots, hankel_rows, pieces)

    blocks = own_block
    for steps in digits(groups):
        arrived = [exchange(blocks, 2, step * bodies) for step in steps]
        blocks = jnp.concatenate([blocks] + arrived, axis=0)
    incoming = pl.pallas_call(
        group_kernel,
        out_shape=shaped((2 * rows, coefs), f32),
        in_specs=[SMEM] + [VMEM] * 3,
        out_specs=VMEM,
        name="group",
    )(group.astype(jnp.int32).reshape(1), blocks, group_maps[0], other_maps)
    for steps in digits(chips):
        message = incoming.astype(bf16)
        for piece in [exchange(message, bodies, 2 * step) for step in steps]:
            incoming += piece.astype(f32)

    message = jnp.where(
        core == 1, incoming, jnp.pad(near[1], ((0, 0), (0, coefs - modes)))
    )
    received = exchange(message, 1, 1)
    incoming = jnp.where(core == 1, incoming, received).astype(bf16)
    near = jnp.where(core == 1, received[:, :modes], near[0])
    return pl.pallas_call(
        last_kernel,
        out_shape=shaped((rows, 2 * modes), f32),
        in_specs=[VMEM] * 4,
        out_specs=VMEM,
        name="last",
    )(incoming, near, down_maps[0], exciting[0])[None]


def solution(mesh):
    return jax.shard_map(
        functools.partial(local, mesh.shape["grp"], mesh.shape["body"]),
        mesh=mesh,
        in_specs=(
            P(("grp", "body"), None, None),
            P(("grp", "body"), None, None),
            P(("grp", "body"), None, None, None),
            P(),
            P(("grp", "body"), None),
            P("grp"),
            P(("grp", "body"), None, None, None),
            P(("grp", "body"), None, None, None),
            P("grp", None, None, "body", None),
        ),
        out_specs=P(("grp", "body"), None, None),
        check_vma=False,
    )
```

time: 121 us -> 36.3 us (0.30)
  blocking collectives: 79.2 us -> 0 us
  local copies, waits for them, and re-layouts: 28.2 us -> 2.19 us
  starting transfers between devices: 0 us -> 12 us
  matrix products: 11.8 us -> 0 us
  Pallas kernels: 0 us -> 9.13 us
  waiting for transfers between devices: 0 us -> 7.09 us
  other arithmetic: 0.96 us -> 5.51 us
    psum x2 -> x0, blocking collectives: 57.1 us -> none  [the longest x1 30.7 us: local(): expansion = lax.psum(partial_value, 'body').astype(jnp.bfloat16)]
    all_gather x2 -> x0, blocking collectives: 22.1 us -> none  [the longest x1 14 us: local(): piece = lax.all_gather(scattered, 'body', axis=0, tiled=True)]
    reshape x2 -> x0, local copies, waits for them, and re-layouts: 12.2 us -> none  [toeplitz_mats(): window.reshape(sequences.shape[:-1] + (length, 2 * length - 1))]
    ppermute x0 -> x12, starting transfers between devices: none -> 12 us  [exchange(): return lax.ppermute(values, AXES, pairs)]
    dot_general x24 -> x0, matrix products: 11.8 us -> none  [the longest x6 2.97 us: complex_apply(): jnp.einsum(form, imag_values, real_mats, preferred_element_type=jnp.float32)]
    pallas_call x0 -> x4, Pallas kernels: none -> 9.13 us  [the longest x1 2.93 us: local(): pl.pallas_call(near_kernel, out_shape=shaped((2, 2 * rows, modes), f32),...]
    slice x2 -> x0, local copies, waits for them, and re-layouts: 8.67 us -> none  [toeplitz_mats(): window = tiled[..., length:length + length * (2 * length - 1)]]
    ppermute x0 -> x12, waiting for transfers between devices: none -> 7.09 us  [exchange(): return lax.ppermute(values, AXES, pairs)]
  transfers between devices with their start and end apart: 0 -> 12, of which waited for: 0 -> 6; matrix products, arithmetic and copies ran while one was open for 0% -> 9% of each run, Pallas kernels for 0% -> 8%
where the time goes in v1:
time: 36.3 us; the launch traced here: 36 us
  starting transfers between devices  12 us (33%)
  Pallas kernels  9.13 us (25%)
  waiting for transfers between devices  7.09 us (20%)
  other arithmetic  5.51 us (15%)
  local copies, waits for them, and re-layouts  2.19 us (6%)
    ppermute x12, starting transfers between devices, exchange(): return lax.ppermute(values, AXES, pairs)  12 us
    ppermute x12, waiting for transfers between devices, exchange(): return lax.ppermute(values, AXES, pairs)  7.09 us
    pallas_call x1, Pallas kernels, local(): pl.pallas_call(near_kernel, out_shape=shaped((2, 2 * rows, modes), f32),...  2.93 us
    pallas_call x1, Pallas kernels, local(): pl.pallas_call(first_kernel, out_shape=(shaped((2 * rows, modes), bf16),...  2.18 us
    unnamed x12, local copies, waits for them, and re-layouts  2.17 us
    pallas_call x1, Pallas kernels, local(): pl.pallas_call(group_kernel, out_shape=shaped((2 * rows, coefs), f32), in...  2.12 us
    pallas_call x1, Pallas kernels, local(): pl.pallas_call(last_kernel, out_shape=shaped((rows, 2 * modes), f32), in_...  1.9 us
    convert_element_type x1, other arithmetic, local(): message = incoming.astype(bf16)  0.92 us
  transfers between devices with their start and end apart: 12, of which 6 were waited for; matrix products, arithmetic and copies ran while one was open for 9% of the time, Pallas kernels for 8%

profile of v1, /device:TPU:0, one launch (start us, length us, event | category | flops | bytes accessed | tf_op | source)
XLA Modules:
  0.0 36.0 jit_solution(4045388181217169521)
XLA Ops:
  0.0 0.0 copy-start.1
  0.0 2.2 %first.1 = (bf16[32,256]{1,0:T(8,128)(2,1)}, f32[32,512]{1,0:T(8,128)}, f32[32,512]{1,0:T(8,128)}) custom-call(s32[1]{0:T(128)} %bitcast.1.core, bf16[16,512]{1,0:T(8,128)(2,1)} %bitcast.50, s32[1,8]{1,0:T(1,128)} %offsets.1, bf16[2,256,256]{2,1,0:T(8,128)(2,1)} %bitcast.46, bf16[2,256,512]{2,1,0:T(8,128)(2,1)} %bitcast.42), custom_call_target="tpu_custom_call" | custom-call | tf_op jit(solution)/shard_map/first/pallas_call | solution.py:137
  2.2 0.5 %collective-permute-start = (f32[32,512]{1,0:T(8,128)}, f32[32,512]{1,0:T(8,128)S(1)}, u32[]{:S(2)}, u32[]{:S(2)}) collective-permute-start(f32[32,512]{1,0:T(8,128)} %get-tuple-element.9), channel_id=1, source_target_pairs={{0,1},{1,0},{2,3},{3,2},{4,5},{5,4},{6,7},{7,6},{8,9},{9,8},{10,11... | collective-permute-start | bytes 196616 | tf_op jit(solution)/shard_map/ppermute | solution.py:130
  2.7 0.0 copy-done.1
  2.7 0.1 collective-permute-start.7
  2.7 0.6 %pad_add_fusion.1.where = s32[2]{0:T(128)} fusion(s32[1]{0:T(128)} %bitcast.17, s32[1]{0:T(128)} %bitcast.1.core), kind=kLoop, calls=%fused_computation.37 | loop fusion | flops 2 | bytes 16 | tf_op jit(solution)/shard_map/stack | solution.py:172
  3.3 0.5 %collective-permute-done = f32[32,512]{1,0:T(8,128)S(1)} collective-permute-done((f32[32,512]{1,0:T(8,128)}, f32[32,512]{1,0:T(8,128)S(1)}, u32[]{:S(2)}, u32[]{:S(2)}) %collective-permute-start) | collective-permute-done | bytes 65568 | tf_op jit(solution)/shard_map/ppermute | solution.py:130
  3.8 0.8 %fusion.10 = (bf16[32,512]{1,0:T(8,128)(2,1)S(1)}, f32[32,512]{1,0:T(8,128)S(1)}) fusion(f32[32,512]{1,0:T(8,128)} %get-tuple-element.8, f32[32,512]{1,0:T(8,128)S(1)} %collective-permute-done), kind=kLoop, calls=%fused_computation.38 | loop fusion | flops 32768 | bytes 229376 | tf_op jit(solution)/shard_map/convert.6
  4.7 0.0 copy-start.4
  4.7 0.7 %copy-done.4 = bf16[32,256]{1,0:T(8,128)(2,1)S(1)} copy-done((bf16[32,256]{1,0:T(8,128)(2,1)S(1)}, bf16[32,256]{1,0:T(8,128)(2,1)}, u32[]{:S(2)}) %copy-start.4) | copy-done | bytes 16408
  5.4 5.0 %collective-permute-start.3 = (bf16[1,2,32,256]{3,2,1,0:T(8,128)(2,1)S(1)}, bf16[1,2,32,256]{3,2,1,0:T(8,128)(2,1)S(1)}, u32[]{:S(2)}, u32[]{:S(2)}) collective-permute-start(bf16[1,2,32,256]{3,2,1,0:T(8,128)(2,1)S(1)} %maximum_select_fusion), channel_id=1, source_target_pairs={{0,6},{1,7},{2,4},{3,5},{4,2},{5,3},{6,0},{7,1},{8,14},{9,15},{10,... | collective-permute-start | bytes 98312 | tf_op jit(solution)/shard_map/ppermute | solution.py:130
  10.4 0.0 collective-permute-start.2
  10.4 0.6 %collective-permute-start.1 = (bf16[1,2,32,256]{3,2,1,0:T(8,128)(2,1)S(1)}, bf16[1,2,32,256]{3,2,1,0:T(8,128)(2,1)S(1)}, u32[]{:S(2)}, u32[]{:S(2)}) collective-permute-start(bf16[1,2,32,256]{3,2,1,0:T(8,128)(2,1)S(1)} %maximum_select_fusion), channel_id=1, source_target_pairs={{0,2},{1,3},{2,0},{3,1},{4,6},{5,7},{6,4},{7,5},{8,10},{9,11},{10,... | collective-permute-start | bytes 98312 | tf_op jit(solution)/shard_map/ppermute | solution.py:130
  11.0 0.0 copy-start.5
  11.0 0.6 %copy-done.5 = s32[1,8]{1,0:T(1,128)S(1)} copy-done((s32[1,8]{1,0:T(1,128)S(1)}, s32[1,8]{1,0:T(1,128)}, u32[]{:S(2)}) %copy-start.5) | copy-done | bytes 56
  11.7 0.6 %pad_add_fusion.offsets = s32[2,8]{1,0:T(2,128)} fusion(s32[1,8]{1,0:T(1,128)S(1)} %slice_convert_fusion.1, s32[1,8]{1,0:T(1,128)S(1)} %copy-done.5), kind=kLoop, calls=%fused_computation.35 | loop fusion | flops 16 | bytes 128 | tf_op jit(solution)/shard_map/concatenate | solution.py:152
  12.3 0.0 collective-permute-done.3
  12.3 2.9 %collective-permute-done.2 = bf16[1,2,32,256]{3,2,1,0:T(8,128)(2,1)S(1)} collective-permute-done((bf16[1,2,32,256]{3,2,1,0:T(8,128)(2,1)S(1)}, bf16[1,2,32,256]{3,2,1,0:T(8,128)(2,1)S(1)}, u32[]{:S(2)}, u32[]{:S(2)}) %collective-permute-start.2) | collective-permute-done | bytes 32800 | tf_op jit(solution)/shard_map/ppermute | solution.py:130
  15.2 0.0 collective-permute-done.1
  15.3 0.1 collective-permute-start.6
  15.3 2.0 %collective-permute-start.5 = (bf16[1,32,128]{2,1,0:T(8,128)(2,1)S(1)}, bf16[1,32,128]{2,1,0:T(8,128)(2,1)S(1)}, u32[]{:S(2)}, u32[]{:S(2)}) collective-permute-start(bf16[1,32,128]{2,1,0:T(8,128)(2,1)S(1)} %fusion.4), channel_id=1, source_target_pairs={{0,2},{1,17},{2,0},{3,19},{4,6},{5,21},{6,4},{7,23},{8,10},{9,25},... | collective-permute-start | bytes 24584 | tf_op jit(solution)/shard_map/ppermute | solution.py:130
  17.3 0.1 collective-permute-start.4
  17.4 0.7 %pad_maximum_fusion.pieces = bf16[4,2,32,256]{3,2,1,0:T(8,128)(2,1)} fusion(bf16[1,2,32,256]{3,2,1,0:T(8,128)(2,1)S(1)} %collective-permute-done.3, bf16[1,2,32,256]{3,2,1,0:T(8,128)(2,1)S(1)} %collective-permute-done.2, bf16[1,2,32,256]{3,2,1,0:T(8,128)(2,1)S(1)} %collective-permute-done.1, bf16[1,2,32,256]{3,2,1,0:T(8,128)(2,1)S(1)} %maximum_bitcast_fusion), kind=kLoop, calls=%fused_computation | loop fusion | flops 196608 | bytes 262144 | tf_op jit(solution)/shard_map/concatenate | solution.py:162
  18.1 2.9 %near.1 = f32[2,32,256]{2,1,0:T(8,128)} custom-call(s32[2]{0:T(128)} %pad_add_fusion.1.where, s32[2,8]{1,0:T(2,128)} %pad_add_fusion.offsets, s32[8]{0:T(128)} %slots.1, bf16[225,2,512]{2,1,0:T(2,128)(2,1)} %table.1, bf16[4,2,32,256]{3,2,1,0:T(8,128)(2,1)} %pad_maximum_fusion.pieces), custom_call_target="tpu_custom_call" | custom-call | tf_op jit(solution)/shard_map/near/pallas_call | solution.py:166
  21.0 0.0 collective-permute-done.6
  21.0 0.0 collective-permute-done.5
  21.0 0.0 collective-permute-done.4
  21.0 0.6 %pad_maximum_fusion.1.pieces = bf16[4,32,128]{2,1,0:T(8,128)(2,1)} fusion(bf16[1,32,128]{2,1,0:T(8,128)(2,1)S(1)} %collective-permute-done.6, bf16[1,32,128]{2,1,0:T(8,128)(2,1)S(1)} %collective-permute-done.5, bf16[1,32,128]{2,1,0:T(8,128)(2,1)S(1)} %collective-permute-done.4, bf16[1,32,128]{2,1,0:T(8,128)(2,1)S(1)} %fusion.4), kind=kLoop, calls=%fused_computation.15 | loop fusion | flops 49152 | bytes 65536 | tf_op jit(solution)/shard_map/concatenate | solution.py:177
  21.7 0.0 collective-permute-done.7.other_maps
  21.7 0.0 copy-start.2
  21.7 0.8 %copy-done.2 = bf16[4,2,64,512]{3,2,1,0:T(8,128)(2,1)} copy-done((bf16[4,2,64,512]{3,2,1,0:T(8,128)(2,1)}, bf16[4,2,64,512]{3,2,1,0:T(8,128)(2,1)S(1)}, u32[]{:S(2)}) %copy-start.2) | copy-done | bytes 524312
  22.5 0.0 copy-start.3
  22.5 2.1 %group.1 = f32[32,512]{1,0:T(8,128)} custom-call(s32[1]{0:T(128)} %bitcast.where, bf16[4,32,128]{2,1,0:T(8,128)(2,1)} %pad_maximum_fusion.1.pieces, bf16[4,2,64,512]{3,2,1,0:T(8,128)(2,1)} %bitcast.44, bf16[4,2,64,512]{3,2,1,0:T(8,128)(2,1)} %copy-done.2), custom_call_target="tpu_custom_call" | custom-call | tf_op jit(solution)/shard_map/group/pallas_call | solution.py:178
  24.6 0.0 copy-start
  24.6 0.9 %convert_element_type.45 = bf16[32,512]{1,0:T(8,128)(2,1)S(1)} convert(f32[32,512]{1,0:T(8,128)} %group.1) | non-fusion elementwise | flops 16384 | bytes 98304 | tf_op jit(solution)/shard_map/convert_element_type | solution.py:186
  25.5 1.5 %collective-permute-start.10 = (bf16[32,512]{1,0:T(8,128)(2,1)S(1)}, bf16[32,512]{1,0:T(8,128)(2,1)S(1)}, u32[]{:S(2)}, u32[]{:S(2)}) collective-permute-start(bf16[32,512]{1,0:T(8,128)(2,1)S(1)} %convert_element_type.45), channel_id=1, source_target_pairs={{0,8},{1,7},{2,10},{3,5},{4,12},{5,3},{6,14},{7,1},{8,0},{9,15},{1... | collective-permute-start | bytes 98312 | tf_op jit(solution)/shard_map/ppermute | solution.py:130
  27.0 0.5 %collective-permute-start.9 = (bf16[32,512]{1,0:T(8,128)(2,1)S(1)}, bf16[32,512]{1,0:T(8,128)(2,1)S(1)}, u32[]{:S(2)}, u32[]{:S(2)}) collective-permute-start(bf16[32,512]{1,0:T(8,128)(2,1)S(1)} %convert_element_type.45), channel_id=1, source_target_pairs={{0,8},{1,5},{2,10},{3,7},{4,12},{5,1},{6,14},{7,3},{8,0},{9,13},{1... | collective-permute-start | bytes 98312 | tf_op jit(solution)/shard_map/ppermute | solution.py:130
  27.5 1.5 %collective-permute-start.8 = (bf16[32,512]{1,0:T(8,128)(2,1)S(1)}, bf16[32,512]{1,0:T(8,128)(2,1)S(1)}, u32[]{:S(2)}, u32[]{:S(2)}) collective-permute-start(bf16[32,512]{1,0:T(8,128)(2,1)S(1)} %convert_element_type.45), channel_id=1, source_target_pairs={{0,8},{1,3},{2,10},{3,1},{4,12},{5,7},{6,14},{7,5},{8,0},{9,11},{1... | collective-permute-start | bytes 98312 | tf_op jit(solution)/shard_map/ppermute | solution.py:130
  29.0 0.0 copy-done.3
  29.0 0.4 %collective-permute-done.10 = bf16[32,512]{1,0:T(8,128)(2,1)S(1)} collective-permute-done((bf16[32,512]{1,0:T(8,128)(2,1)S(1)}, bf16[32,512]{1,0:T(8,128)(2,1)S(1)}, u32[]{:S(2)}, u32[]{:S(2)}) %collective-permute-start.10) | collective-permute-done | bytes 32800 | tf_op jit(solution)/shard_map/ppermute | solution.py:130
  29.4 1.5 %collective-permute-done.9 = bf16[32,512]{1,0:T(8,128)(2,1)S(1)} collective-permute-done((bf16[32,512]{1,0:T(8,128)(2,1)S(1)}, bf16[32,512]{1,0:T(8,128)(2,1)S(1)}, u32[]{:S(2)}, u32[]{:S(2)}) %collective-permute-start.9) | collective-permute-done | bytes 32800 | tf_op jit(solution)/shard_map/ppermute | solution.py:130
  30.9 0.5 %collective-permute-done.8 = bf16[32,512]{1,0:T(8,128)(2,1)S(1)} collective-permute-done((bf16[32,512]{1,0:T(8,128)(2,1)S(1)}, bf16[32,512]{1,0:T(8,128)(2,1)S(1)}, u32[]{:S(2)}, u32[]{:S(2)}) %collective-permute-start.8) | collective-permute-done | bytes 32800 | tf_op jit(solution)/shard_map/ppermute | solution.py:130
  31.5 0.0 copy-done
  31.5 0.1 collective-permute-start.11
  31.6 1.2 %collective-permute-done.11 = f32[32,512]{1,0:T(8,128)S(1)} collective-permute-done((f32[32,512]{1,0:T(8,128)S(1)}, f32[32,512]{1,0:T(8,128)S(1)}, u32[]{:S(2)}, u32[]{:S(2)}) %collective-permute-start.11) | collective-permute-done | bytes 65568 | tf_op jit(solution)/shard_map/ppermute | solution.py:130
  32.8 0.6 %select_convert_fusion.incoming = bf16[32,512]{1,0:T(8,128)(2,1)} fusion(f32[32,512]{1,0:T(8,128)S(1)} %collective-permute-done.11, pred[]{:T(512)S(6)} %eq.4, bf16[32,512]{1,0:T(8,128)(2,1)S(1)} %collective-permute-done.10, bf16[32,512]{1,0:T(8,128)(2,1)S(1)} %collective-permute-done.9, f32[32,512]{1,0:T(8,128)S(1)} %copy-done, ...), kind=kLoop, calls=%fused_computation.1 | loop fusion | flops 114688 | bytes 262145 | tf_op jit(solution)/shard_map/convert_element_type | solution.py:194
  33.4 0.6 %fusion.near = f32[32,256]{1,0:T(8,128)} fusion(f32[2,32,256]{2,1,0:T(8,128)S(1)} %copy-done.3, f32[32,512]{1,0:T(8,128)S(1)} %collective-permute-done.11, pred[]{:T(512)S(6)} %eq.4), kind=kLoop, calls=%fused_computation.5 | loop fusion | flops 8192 | bytes 98305 | tf_op jit(solution)/shard_map/jit(_where)/select_n | solution.py:195
  34.1 1.9 %last.1 = f32[16,512]{1,0:T(8,128)} custom-call(bf16[32,512]{1,0:T(8,128)(2,1)} %select_convert_fusion.incoming, f32[32,256]{1,0:T(8,128)} %fusion.near, bf16[2,512,256]{2,1,0:T(8,128)(2,1)} %bitcast.43, f32[16,512]{1,0:T(8,128)} %bitcast.49), custom_call_target="tpu_custom_call" | custom-call | tf_op jit(solution)/shard_map/last/pallas_call | solution.py:196
  (11 shorter events, 0.1 us)
Async XLA Ops:
  0.0 2.7 %copy-start.1 = (bf16[1,4,2,64,512]{4,3,2,1,0:T(8,128)(2,1)S(1)}, bf16[1,4,2,64,512]{4,3,2,1,0:T(8,128)(2,1)}, u32[]{:S(2)}) copy-start(bf16[1,4,2,64,512]{4,3,2,1,0:T(8,128)(2,1)} %param.17) | copy-start | bytes 1572868
  2.2 1.6 %collective-permute-start = (f32[32,512]{1,0:T(8,128)}, f32[32,512]{1,0:T(8,128)S(1)}, u32[]{:S(2)}, u32[]{:S(2)}) collective-permute-start(f32[32,512]{1,0:T(8,128)} %get-tuple-element.9), channel_id=1, source_target_pairs={{0,1},{1,0},{2,3},{3,2},{4,5},{5,4},{6,7},{7,6},{8,9},{9,8},{10,11... | collective-permute-start | bytes 196616 | tf_op jit(solution)/shard_map/ppermute | solution.py:130
  2.7 19.0 %collective-permute-start.7 = (bf16[4,2,64,512]{3,2,1,0:T(8,128)(2,1)S(1)}, bf16[4,2,64,512]{3,2,1,0:T(8,128)(2,1)S(1)}, u32[]{:S(2)}, u32[]{:S(2)}) collective-permute-start(bf16[4,2,64,512]{3,2,1,0:T(8,128)(2,1)S(1)} %bitcast.45), channel_id=1, source_target_pairs={{0,1},{1,0},{2,3},{3,2},{4,5},{5,4},{6,7},{7,6},{8,9},{9,8},{10,11... | collective-permute-start | bytes 1572872 | tf_op jit(solution)/shard_map/ppermute | solution.py:130
  4.7 0.7 %copy-start.4 = (bf16[32,256]{1,0:T(8,128)(2,1)S(1)}, bf16[32,256]{1,0:T(8,128)(2,1)}, u32[]{:S(2)}) copy-start(bf16[32,256]{1,0:T(8,128)(2,1)} %get-tuple-element.10) | copy-start | bytes 49156
  5.4 6.9 %collective-permute-start.3 = (bf16[1,2,32,256]{3,2,1,0:T(8,128)(2,1)S(1)}, bf16[1,2,32,256]{3,2,1,0:T(8,128)(2,1)S(1)}, u32[]{:S(2)}, u32[]{:S(2)}) collective-permute-start(bf16[1,2,32,256]{3,2,1,0:T(8,128)(2,1)S(1)} %maximum_select_fusion), channel_id=1, source_target_pairs={{0,6},{1,7},{2,4},{3,5},{4,2},{5,3},{6,0},{7,1},{8,14},{9,15},{10,... | collective-permute-start | bytes 98312 | tf_op jit(solution)/shard_map/ppermute | solution.py:130
  10.4 4.8 %collective-permute-start.2 = (bf16[1,2,32,256]{3,2,1,0:T(8,128)(2,1)S(1)}, bf16[1,2,32,256]{3,2,1,0:T(8,128)(2,1)S(1)}, u32[]{:S(2)}, u32[]{:S(2)}) collective-permute-start(bf16[1,2,32,256]{3,2,1,0:T(8,128)(2,1)S(1)} %maximum_select_fusion), channel_id=1, source_target_pairs={{0,4},{1,5},{2,6},{3,7},{4,0},{5,1},{6,2},{7,3},{8,12},{9,13},{10,... | collective-permute-start | bytes 98312 | tf_op jit(solution)/shard_map/ppermute | solution.py:130
  10.4 4.8 %collective-permute-start.1 = (bf16[1,2,32,256]{3,2,1,0:T(8,128)(2,1)S(1)}, bf16[1,2,32,256]{3,2,1,0:T(8,128)(2,1)S(1)}, u32[]{:S(2)}, u32[]{:S(2)}) collective-permute-start(bf16[1,2,32,256]{3,2,1,0:T(8,128)(2,1)S(1)} %maximum_select_fusion), channel_id=1, source_target_pairs={{0,2},{1,3},{2,0},{3,1},{4,6},{5,7},{6,4},{7,5},{8,10},{9,11},{10,... | collective-permute-start | bytes 98312 | tf_op jit(solution)/shard_map/ppermute | solution.py:130
  11.0 0.7 %copy-start.5 = (s32[1,8]{1,0:T(1,128)S(1)}, s32[1,8]{1,0:T(1,128)}, u32[]{:S(2)}) copy-start(s32[1,8]{1,0:T(1,128)} %offsets.1) | copy-start | bytes 100
  15.3 5.8 %collective-permute-start.6 = (bf16[1,32,128]{2,1,0:T(8,128)(2,1)S(1)}, bf16[1,32,128]{2,1,0:T(8,128)(2,1)S(1)}, u32[]{:S(2)}, u32[]{:S(2)}) collective-permute-start(bf16[1,32,128]{2,1,0:T(8,128)(2,1)S(1)} %fusion.4), channel_id=1, source_target_pairs={{0,2},{1,25},{2,0},{3,27},{4,6},{5,29},{6,4},{7,31},{8,10},{9,17},... | collective-permute-start | bytes 24584 | tf_op jit(solution)/shard_map/ppermute | solution.py:130
  15.3 5.7 %collective-permute-start.5 = (bf16[1,32,128]{2,1,0:T(8,128)(2,1)S(1)}, bf16[1,32,128]{2,1,0:T(8,128)(2,1)S(1)}, u32[]{:S(2)}, u32[]{:S(2)}) collective-permute-start(bf16[1,32,128]{2,1,0:T(8,128)(2,1)S(1)} %fusion.4), channel_id=1, source_target_pairs={{0,2},{1,17},{2,0},{3,19},{4,6},{5,21},{6,4},{7,23},{8,10},{9,25},... | collective-permute-start | bytes 24584 | tf_op jit(solution)/shard_map/ppermute | solution.py:130
  17.3 3.7 %collective-permute-start.4 = (bf16[1,32,128]{2,1,0:T(8,128)(2,1)S(1)}, bf16[1,32,128]{2,1,0:T(8,128)(2,1)S(1)}, u32[]{:S(2)}, u32[]{:S(2)}) collective-permute-start(bf16[1,32,128]{2,1,0:T(8,128)(2,1)S(1)} %fusion.4), channel_id=1, source_target_pairs={{0,2},{1,9},{2,0},{3,11},{4,6},{5,13},{6,4},{7,15},{8,10},{9,1},{1... | collective-permute-start | bytes 24584 | tf_op jit(solution)/shard_map/ppermute | solution.py:130
  21.7 0.8 %copy-start.2 = (bf16[4,2,64,512]{3,2,1,0:T(8,128)(2,1)}, bf16[4,2,64,512]{3,2,1,0:T(8,128)(2,1)S(1)}, u32[]{:S(2)}) copy-start(bf16[4,2,64,512]{3,2,1,0:T(8,128)(2,1)S(1)} %collective-permute-done.7.other_maps) | copy-start | bytes 1572868
  22.5 6.6 %copy-start.3 = (f32[2,32,256]{2,1,0:T(8,128)S(1)}, f32[2,32,256]{2,1,0:T(8,128)}, u32[]{:S(2)}) copy-start(f32[2,32,256]{2,1,0:T(8,128)} %near.1) | copy-start | bytes 196612
  24.6 6.9 %copy-start = (f32[32,512]{1,0:T(8,128)S(1)}, f32[32,512]{1,0:T(8,128)}, u32[]{:S(2)}) copy-start(f32[32,512]{1,0:T(8,128)} %group.1) | copy-start | bytes 196612
  25.5 3.9 %collective-permute-start.10 = (bf16[32,512]{1,0:T(8,128)(2,1)S(1)}, bf16[32,512]{1,0:T(8,128)(2,1)S(1)}, u32[]{:S(2)}, u32[]{:S(2)}) collective-permute-start(bf16[32,512]{1,0:T(8,128)(2,1)S(1)} %convert_element_type.45), channel_id=1, source_target_pairs={{0,8},{1,7},{2,10},{3,5},{4,12},{5,3},{6,14},{7,1},{8,0},{9,15},{1... | collective-permute-start | bytes 98312 | tf_op jit(solution)/shard_map/ppermute | solution.py:130
  27.0 3.9 %collective-permute-start.9 = (bf16[32,512]{1,0:T(8,128)(2,1)S(1)}, bf16[32,512]{1,0:T(8,128)(2,1)S(1)}, u32[]{:S(2)}, u32[]{:S(2)}) collective-permute-start(bf16[32,512]{1,0:T(8,128)(2,1)S(1)} %convert_element_type.45), channel_id=1, source_target_pairs={{0,8},{1,5},{2,10},{3,7},{4,12},{5,1},{6,14},{7,3},{8,0},{9,13},{1... | collective-permute-start | bytes 98312 | tf_op jit(solution)/shard_map/ppermute | solution.py:130
  27.5 3.9 %collective-permute-start.8 = (bf16[32,512]{1,0:T(8,128)(2,1)S(1)}, bf16[32,512]{1,0:T(8,128)(2,1)S(1)}, u32[]{:S(2)}, u32[]{:S(2)}) collective-permute-start(bf16[32,512]{1,0:T(8,128)(2,1)S(1)} %convert_element_type.45), channel_id=1, source_target_pairs={{0,8},{1,3},{2,10},{3,1},{4,12},{5,7},{6,14},{7,5},{8,0},{9,11},{1... | collective-permute-start | bytes 98312 | tf_op jit(solution)/shard_map/ppermute | solution.py:130
  31.5 1.3 %collective-permute-start.11 = (f32[32,512]{1,0:T(8,128)S(1)}, f32[32,512]{1,0:T(8,128)S(1)}, u32[]{:S(2)}, u32[]{:S(2)}) collective-permute-start(f32[32,512]{1,0:T(8,128)S(1)} %pad_select_fusion), channel_id=1, source_target_pairs={{0,1},{1,0},{2,3},{3,2},{4,5},{5,4},{6,7},{7,6},{8,9},{9,8},{10,11... | collective-permute-start | bytes 196616 | tf_op jit(solution)/shard_map/ppermute | solution.py:130

commit v2 on v1

v2 whole, which is shorter than its diff:
```python
import functools

import jax
import jax.numpy as jnp
from jax import lax
from jax.experimental import pallas as pl
from jax.experimental.pallas import tpu as pltpu
from jax.sharding import PartitionSpec as P

AXES = ("grp", "body")
SMEM = pl.BlockSpec(memory_space=pltpu.SMEM)
VMEM = pl.BlockSpec(memory_space=pltpu.VMEM)
HBM = pl.BlockSpec(memory_space=pltpu.HBM)
PARAMS = pltpu.CompilerParams(vmem_limit_bytes=8 << 20)
BF16, F32 = jnp.bfloat16, jnp.float32


def crossed(values):
    rows = values.shape[0] // 2
    real, imag = values[:rows], values[rows:]
    return jnp.concatenate(
        [jnp.concatenate([real, -imag], axis=1), jnp.concatenate([imag, real], axis=1)], axis=0
    )


def dot(left, right):
    return jnp.dot(left, right, preferred_element_type=F32)


def shaped(shape, dtype):
    return jax.ShapeDtypeStruct(shape, dtype)


def in_hbm(*arrays):
    return [pltpu.with_memory_space_constraint(array, pltpu.HBM) for array in arrays]


def first_kernel(
    incident_hbm, offsets_hbm, t_hbm, up_hbm, scattered, message, incident, offsets, t_mats, up, sems
):
    sources = (incident_hbm, t_hbm, offsets_hbm, up_hbm)
    targets = (incident, t_mats, offsets, up)
    copies = [
        pltpu.make_async_copy(source, target, sems.at[i])
        for i, (source, target) in enumerate(zip(sources, targets))
    ]
    for copy in copies:
        copy.start()
    modes, coefs = up.shape[1:]
    rows = 2 * incident.shape[0]
    copies[0].wait()
    values = jnp.concatenate([incident[:, :modes], incident[:, modes:]], axis=0)
    values = crossed(values)
    copies[1].wait()
    own = dot(values, t_mats[...].reshape(2 * modes, modes)).astype(BF16)
    scattered[...] = own
    message[:rows, coefs:] = own.astype(F32)
    copies[2].wait()
    message[rows:, :] = jnp.zeros((message.shape[0] - rows, coefs + modes), F32)
    message[rows : rows + 1, : offsets.shape[1]] = offsets[...].astype(F32)
    own = crossed(own)
    copies[3].wait()
    message[:rows, :coefs] = dot(own, up[...].reshape(2 * modes, coefs))


def first_call(incident, offsets, t_mats, up):
    rows, modes, coefs = 2 * incident.shape[0], up.shape[1], up.shape[2]
    return pl.pallas_call(
        first_kernel,
        out_shape=(
            shaped((rows, modes), BF16),
            shaped((rows + 8, coefs + modes), F32),
        ),
        in_specs=[HBM] * 4,
        out_specs=(VMEM, VMEM),
        scratch_shapes=[
            pltpu.VMEM(incident.shape, BF16),
            pltpu.VMEM(offsets.shape, jnp.int32),
            pltpu.VMEM(t_mats.shape, BF16),
            pltpu.VMEM(up.shape, BF16),
            pltpu.SemaphoreType.DMA((4,)),
        ],
        compiler_params=PARAMS,
        name="first",
    )(*in_hbm(incident, offsets, t_mats, up))


def near_kernel(places, members, core, chip, indices, exciting_hbm, table, *rest):
    pieces, (near, exciting, sem) = rest[:-3], rest[-3:]
    copy = pltpu.make_async_copy(exciting_hbm, exciting, sem)
    copy.start()
    _, rows, modes = near.shape
    half = modes // 2

    @pl.when(core[0] == 1)
    def _():
        for column in range(2):
            total = jnp.zeros((rows, 2 * modes), F32)
            for other, piece, lane in places:
                for member in range(2):
                    if other == 0 and member == column:
                        continue
                    source = (chip[0] ^ other) * 2 + member
                    slot = indices[2 * members + source]
                    sequence = table[indices[column * members + slot]].astype(F32)
                    mats = []
                    for part in range(2):
                        band = jnp.broadcast_to(sequence[part : part + 1], (half, 2 * modes))
                        band = pltpu.roll(band, 0, 1, stride=1, stride_axis=0)
                        band = band.astype(BF16)
                        mats.append(
                            jnp.concatenate(
                                [band[:, modes:], band[:, half : half + modes]], axis=0
                            )
                        )
                    start = lane + member * modes
                    values = pieces[piece][:, start : start + modes]
                    total += dot(values, jnp.concatenate(mats, axis=1))
            top, low = total[: rows // 2], total[rows // 2 :]
            near[column, : rows // 2, :] = top[:, :modes] - low[:, modes:]
            near[column, rows // 2 :, :] = top[:, modes:] + low[:, :modes]

    copy.wait()


def group_kernel(places, group, own_maps, other_maps, *rest):
    pieces, incoming = rest[:-1], rest[-1]
    total = jnp.zeros(incoming.shape, F32)
    for other, piece, index in places:
        source = group[0] ^ other
        mats = jnp.concatenate(
            [other_maps[source, 0], own_maps[source, 0], other_maps[source, 1], own_maps[source, 1]],
            axis=0,
        )
        total += dot(crossed(pieces[piece][index]), mats)
    incoming[...] = total


def last_kernel(core, incoming, near, received, down, exciting, updated):
    coefs, modes = down.shape[1:]
    rows = exciting.shape[0]

    def finish(values, close):
        far = dot(crossed(values.astype(BF16)), down[...].reshape(2 * coefs, modes)) + close
        updated[:, :modes] = exciting[:, :modes] + far[:rows]
        updated[:, modes:] = exciting[:, modes:] + far[rows:]

    @pl.when(core[0] == 0)
    def _():
        finish(received[:, :coefs], received[:, coefs:])

    @pl.when(core[0] == 1)
    def _():
        finish(incoming[...], near[1])


def digits(count):
    bits = count.bit_length() - 1
    found = []
    while bits > 0:
        shift = bits - 2 if bits >= 2 else 0
        found.append([k << shift for k in range((1 << (bits - shift)) - 1, 0, -1)])
        bits = shift
    return found


def local(
    groups,
    bodies,
    incident,
    exciting,
    t_matrices,
    hankel_rows,
    offsets,
    lattice_slots,
    up_maps,
    down_maps,
    group_maps,
):
    body = lax.axis_index("body")
    group = lax.axis_index("grp")
    core, chip = body & 1, body >> 1
    chips = bodies // 2
    modes, coefs = up_maps.shape[2:]

    def exchange(values, even, odd):
        pairs = [(i, i ^ (odd if i % 2 else even)) for i in range(groups * bodies)]
        return lax.ppermute(values, AXES, pairs)

    core_at, chip_at, group_at = (x.astype(jnp.int32).reshape(1) for x in (core, chip, group))
    scattered, message = first_call(incident[0], offsets, t_matrices[0], up_maps[0])
    rows = scattered.shape[0]
    received = exchange(message, 1, 1)
    other_maps = exchange(group_maps[0], 1, 1)

    expansion = message[:rows, :coefs] + received[:rows, :coefs]
    members = offsets.shape[1]
    indices = jnp.concatenate(
        [received[rows, :members].astype(jnp.int32), offsets[0], lattice_slots], axis=0
    )
    pieces = [jnp.concatenate([received[:rows, coefs:].astype(BF16), scattered], axis=1)]
    places = [(0, 0, 0)]
    aside = bodies if groups > 1 else 2
    for steps in digits(chips):
        width = expansion.shape[1] // (len(steps) + 1)
        unit = min(steps)
        own = (chip // unit) % (len(steps) + 1)

        def part(index):
            return lax.dynamic_slice_in_dim(expansion, index * width, width, 1)

        gathered = [pieces[p][:, lane : lane + 2 * modes] for _, p, lane in places]
        messages = [
            jnp.concatenate(gathered + [part(own ^ (step // unit)).astype(BF16)], axis=1)
            for step in steps
        ]
        arrived = [exchange(m, aside, 2 * step) for m, step in zip(messages, steps)]
        held = len(places)
        expansion = part(own)
        for step, piece in zip(steps, arrived):
            expansion += piece[:, 2 * modes * held :].astype(F32)
            places += [
                (other ^ step, len(pieces), 2 * modes * i)
                for i, (other, _, _) in enumerate(places[:held])
            ]
            pieces.append(piece)

    near, exciting_near = pl.pallas_call(
        functools.partial(near_kernel, tuple(places), members),
        out_shape=(shaped((2, rows, modes), F32), shaped(exciting.shape[1:], F32)),
        in_specs=[SMEM] * 3 + [HBM, VMEM] + [VMEM] * len(pieces),
        out_specs=(VMEM, VMEM),
        scratch_shapes=[pltpu.SemaphoreType.DMA],
        compiler_params=PARAMS,
        name="near",
    )(core_at, chip_at, indices, *in_hbm(exciting[0]), hankel_rows, *pieces)

    blocks = [expansion.astype(BF16)[None]]
    group_places = [(0, 0, 0)]
    for steps in digits(groups):
        message = [blocks[b][i] for _, b, i in group_places]
        message = blocks[0] if len(message) == 1 else jnp.stack(message)
        held = list(group_places)
        for step in reversed(steps):
            group_places += [(other ^ step, len(blocks), i) for i, (other, _, _) in enumerate(held)]
            blocks.append(exchange(message, 2, step * bodies))
    incoming = pl.pallas_call(
        functools.partial(group_kernel, tuple(group_places[1:])),
        out_shape=shaped((rows, coefs), F32),
        in_specs=[SMEM] + [VMEM] * (2 + len(blocks)),
        out_specs=VMEM,
        compiler_params=PARAMS,
        name="group",
    )(group_at, group_maps[0], other_maps, *blocks)

    for steps in digits(chips):
        message = incoming.astype(BF16)
        for piece in [exchange(message, aside, 2 * step) for step in reversed(steps)]:
            incoming += piece.astype(F32)

    received = exchange(jnp.concatenate([incoming, near[0]], axis=1), 1, 1)
    return pl.pallas_call(
        last_kernel,
        out_shape=shaped(exciting.shape[1:], F32),
        in_specs=[SMEM] + [VMEM] * 5,
        out_specs=VMEM,
        compiler_params=PARAMS,
        name="last",
    )(core_at, incoming, near, received, down_maps[0], exciting_near)[None]


def solution(mesh):
    return jax.shard_map(
        functools.partial(local, mesh.shape["grp"], mesh.shape["body"]),
        mesh=mesh,
        in_specs=(
            P(("grp", "body"), None, None),
            P(("grp", "body"), None, None),
            P(("grp", "body"), None, None, None),
            P(),
            P(("grp", "body"), None),
            P("grp"),
            P(("grp", "body"), None, None, None),
            P(("grp", "body"), None, None, None),
            P("grp", None, None, "body", None),
        ),
        out_specs=P(("grp", "body"), None, None),
        check_vma=False,
    )
```

time: 36.3 us -> 24.9 us (0.69)
  other arithmetic: 5.51 us -> 0.16 us
  Pallas kernels: 9.13 us -> 3.81 us
  local copies, waits for them, and re-layouts: 2.19 us -> 0.05 us
  starting transfers between devices: 12 us -> 13.1 us
    pallas_call x4, Pallas kernels: 9.13 us -> 3.81 us  [the longest x1 1.44 us: first_call(): pl.pallas_call(first_kernel, out_shape=(shaped((rows, modes), BF16), shap...]
    unnamed x12 -> x10, local copies, waits for them, and re-layouts: 2.17 us -> 0.03 us
    concatenate x3 -> x4, other arithmetic: 1.85 us -> 0.1 us  [the longest x1 0.08 us: local(): jnp.concatenate([received[rows, :members].astype(jnp.int32), offsets[0],...]
    convert_element_type x3 -> x2, other arithmetic: 1.56 us -> 0.02 us  [the longest x1 0.01 us: local(): message = incoming.astype(BF16)]
    another operation x2 -> x0, other arithmetic: 1.41 us -> none
    ppermute x12, starting transfers between devices: 12 us -> 13.1 us  [exchange(): return lax.ppermute(values, AXES, pairs)]
    select_n x3 -> x0, other arithmetic: 0.65 us -> none  [the longest x1 0.62 us: local(): near = jnp.where(core == 1, received[:, :modes], near[0])]
  transfers between devices with their start and end apart: 12 -> 12, of which waited for: 6 -> 9; matrix products, arithmetic and copies ran while one was open for 9% -> 1% of each run, Pallas kernels for 8% -> 5%
where the time goes in v2:
time: 24.9 us; the launch traced here: 24.7 us
  starting transfers between devices  13.1 us (53%)
  waiting for transfers between devices  7.45 us (30%)
  Pallas kernels  3.81 us (15%)
    ppermute x12, starting transfers between devices, exchange(): return lax.ppermute(values, AXES, pairs)  13.1 us
    ppermute x12, waiting for transfers between devices, exchange(): return lax.ppermute(values, AXES, pairs)  7.45 us
    pallas_call x1, Pallas kernels, first_call(): pl.pallas_call(first_kernel, out_shape=(shaped((rows, modes), BF16), shap...  1.44 us
    pallas_call x1, Pallas kernels, local(): pl.pallas_call(functools.partial(near_kernel, tuple(places), members), ou...  1.31 us
    pallas_call x1, Pallas kernels, local(): pl.pallas_call(last_kernel, out_shape=shaped(exciting.shape[1:], F32), in...  0.82 us
  transfers between devices with their start and end apart: 12, of which 9 were waited for; matrix products, arithmetic and copies ran while one was open for 1% of the time, Pallas kernels for 5%

profile of v2, /device:TPU:0, one launch (start us, length us, event | category | flops | bytes accessed | tf_op | source)
XLA Modules:
  0.0 24.7 jit_solution(5316866350876154650)
XLA Ops:
  0.0 0.0 copy-start
  0.0 1.4 %first.1 = (bf16[32,256]{1,0:T(8,128)(2,1)S(1)}, f32[40,768]{1,0:T(8,128)S(1)}) custom-call(bf16[16,512]{1,0:T(8,128)(2,1)} %bitcast.23, s32[1,8]{1,0:T(1,128)} %offsets_hbm.1, bf16[2,256,256]{2,1,0:T(8,128)(2,1)} %bitcast.21, bf16[2,256,512]{2,1,0:T(8,128)(2,1)} %bitcast.20), custom_call_target="tpu_custom_call" | custom-call | tf_op jit(solution)/shard_map/first/pallas_call | solution.py:68
  1.5 0.0 copy-start.2
  1.5 0.6 %collective-permute-start.1 = (f32[40,768]{1,0:T(8,128)S(1)}, f32[40,768]{1,0:T(8,128)S(1)}, u32[]{:S(2)}, u32[]{:S(2)}) collective-permute-start(f32[40,768]{1,0:T(8,128)S(1)} %get-tuple-element.9), channel_id=1, source_target_pairs={{0,1},{1,0},{2,3},{3,2},{4,5},{5,4},{6,7},{7,6},{8,9},{9,8},{10,11... | collective-permute-start | bytes 368648 | tf_op jit(solution)/shard_map/ppermute | solution.py:188
  2.0 0.0 copy-done
  2.0 0.1 collective-permute-start
  2.1 0.9 %collective-permute-done.1 = f32[40,768]{1,0:T(8,128)S(1)} collective-permute-done((f32[40,768]{1,0:T(8,128)S(1)}, f32[40,768]{1,0:T(8,128)S(1)}, u32[]{:S(2)}, u32[]{:S(2)}) %collective-permute-start.1) | collective-permute-done | bytes 122912 | tf_op jit(solution)/shard_map/ppermute | solution.py:188
  3.1 2.9 %collective-permute-start.2 = (bf16[32,640]{1,0:T(8,128)(2,1)S(1)}, bf16[32,640]{1,0:T(8,128)(2,1)S(1)}, u32[]{:S(2)}, u32[]{:S(2)}) collective-permute-start(bf16[32,640]{1,0:T(8,128)(2,1)S(1)} %get-tuple-element.16), channel_id=1, source_target_pairs={{0,8},{1,7},{2,10},{3,5},{4,12},{5,3},{6,14},{7,1},{8,0},{9,15},{1... | collective-permute-start | bytes 122888 | tf_op jit(solution)/shard_map/ppermute | solution.py:188
  6.0 0.1 collective-permute-start.3
  6.1 1.9 %collective-permute-start.4 = (bf16[32,640]{1,0:T(8,128)(2,1)S(1)}, bf16[32,640]{1,0:T(8,128)(2,1)S(1)}, u32[]{:S(2)}, u32[]{:S(2)}) collective-permute-start(bf16[32,640]{1,0:T(8,128)(2,1)S(1)} %get-tuple-element.18), channel_id=1, source_target_pairs={{0,8},{1,3},{2,10},{3,1},{4,12},{5,7},{6,14},{7,5},{8,0},{9,11},{1... | collective-permute-start | bytes 122888 | tf_op jit(solution)/shard_map/ppermute | solution.py:188
  8.0 0.0 collective-permute-done.2.rest_1_
  8.0 2.0 %collective-permute-done.3.rest_2_ = bf16[32,640]{1,0:T(8,128)(2,1)S(1)} collective-permute-done((bf16[32,640]{1,0:T(8,128)(2,1)S(1)}, bf16[32,640]{1,0:T(8,128)(2,1)S(1)}, u32[]{:S(2)}, u32[]{:S(2)}) %collective-permute-start.3) | collective-permute-done | bytes 40992 | tf_op jit(solution)/shard_map/ppermute | solution.py:188
  10.0 0.4 %collective-permute-done.4.rest_3_ = bf16[32,640]{1,0:T(8,128)(2,1)S(1)} collective-permute-done((bf16[32,640]{1,0:T(8,128)(2,1)S(1)}, bf16[32,640]{1,0:T(8,128)(2,1)S(1)}, u32[]{:S(2)}, u32[]{:S(2)}) %collective-permute-start.4) | collective-permute-done | bytes 40992 | tf_op jit(solution)/shard_map/ppermute | solution.py:188
  10.4 0.0 copy-start.3
  10.4 0.0 copy-start.4
  10.5 1.7 %collective-permute-start.7 = (bf16[1,32,128]{2,1,0:T(8,128)(2,1)S(1)}, bf16[1,32,128]{2,1,0:T(8,128)(2,1)S(1)}, u32[]{:S(2)}, u32[]{:S(2)}) collective-permute-start(bf16[1,32,128]{2,1,0:T(8,128)(2,1)S(1)} %fusion.rest_0_), channel_id=1, source_target_pairs={{0,2},{1,25},{2,0},{3,27},{4,6},{5,29},{6,4},{7,31},{8,10},{9,17},... | collective-permute-start | bytes 24584 | tf_op jit(solution)/shard_map/ppermute | solution.py:188
  12.2 0.4 %collective-permute-start.6 = (bf16[1,32,128]{2,1,0:T(8,128)(2,1)S(1)}, bf16[1,32,128]{2,1,0:T(8,128)(2,1)S(1)}, u32[]{:S(2)}, u32[]{:S(2)}) collective-permute-start(bf16[1,32,128]{2,1,0:T(8,128)(2,1)S(1)} %fusion.rest_0_), channel_id=1, source_target_pairs={{0,2},{1,17},{2,0},{3,19},{4,6},{5,21},{6,4},{7,23},{8,10},{9,25},... | collective-permute-start | bytes 24584 | tf_op jit(solution)/shard_map/ppermute | solution.py:188
  12.5 1.7 %collective-permute-start.5 = (bf16[1,32,128]{2,1,0:T(8,128)(2,1)S(1)}, bf16[1,32,128]{2,1,0:T(8,128)(2,1)S(1)}, u32[]{:S(2)}, u32[]{:S(2)}) collective-permute-start(bf16[1,32,128]{2,1,0:T(8,128)(2,1)S(1)} %fusion.rest_0_), channel_id=1, source_target_pairs={{0,2},{1,9},{2,0},{3,11},{4,6},{5,13},{6,4},{7,15},{8,10},{9,1},{1... | collective-permute-start | bytes 24584 | tf_op jit(solution)/shard_map/ppermute | solution.py:188
  14.2 0.0 copy-done.3
  14.2 0.0 copy-done.4
  14.2 0.1 pad_add_fusion.indices
  14.3 0.0 copy-done.2
  14.3 1.3 %near.1 = (f32[2,32,256]{2,1,0:T(8,128)S(1)}, f32[16,512]{1,0:T(8,128)S(1)}) custom-call(s32[1]{0:T(128)} %bitcast.core, s32[1]{0:T(128)} %bitcast.7.chip, s32[24]{0:T(128)S(1)} %pad_add_fusion.indices, f32[16,512]{1,0:T(8,128)} %bitcast.22, bf16[225,2,512]{2,1,0:T(2,128)(2,1)S(1)} %copy-done.2, bf16[32,512]{1,0:T(8,128)(2,1)S(1)} %pad_maximum_fusion.5.rest_0_, ...), custom_call_target="tpu_custom_call" | custom-call | tf_op jit(solution)/shard_map/near/pallas_call | solution.py:228
  15.6 0.0 collective-permute-done.7.rest_3_
  15.6 0.2 collective-permute-done.6.rest_2_
  15.8 0.4 %collective-permute-done.5.rest_1_ = bf16[1,32,128]{2,1,0:T(8,128)(2,1)S(1)} collective-permute-done((bf16[1,32,128]{2,1,0:T(8,128)(2,1)S(1)}, bf16[1,32,128]{2,1,0:T(8,128)(2,1)S(1)}, u32[]{:S(2)}, u32[]{:S(2)}) %collective-permute-start.5) | collective-permute-done | bytes 8224 | tf_op jit(solution)/shard_map/ppermute | solution.py:188
  16.2 0.0 collective-permute-done.other_maps
  16.2 0.2 group.1
  16.4 0.0 copy-start.1
  16.5 1.7 %collective-permute-start.10 = (bf16[32,512]{1,0:T(8,128)(2,1)S(1)}, bf16[32,512]{1,0:T(8,128)(2,1)S(1)}, u32[]{:S(2)}, u32[]{:S(2)}) collective-permute-start(bf16[32,512]{1,0:T(8,128)(2,1)S(1)} %convert_element_type.47), channel_id=1, source_target_pairs={{0,8},{1,7},{2,10},{3,5},{4,12},{5,3},{6,14},{7,1},{8,0},{9,15},{1... | collective-permute-start | bytes 98312 | tf_op jit(solution)/shard_map/ppermute | solution.py:188
  18.1 0.4 %collective-permute-start.9 = (bf16[32,512]{1,0:T(8,128)(2,1)S(1)}, bf16[32,512]{1,0:T(8,128)(2,1)S(1)}, u32[]{:S(2)}, u32[]{:S(2)}) collective-permute-start(bf16[32,512]{1,0:T(8,128)(2,1)S(1)} %convert_element_type.47), channel_id=1, source_target_pairs={{0,8},{1,5},{2,10},{3,7},{4,12},{5,1},{6,14},{7,3},{8,0},{9,13},{1... | collective-permute-start | bytes 98312 | tf_op jit(solution)/shard_map/ppermute | solution.py:188
  18.6 1.6 %collective-permute-start.8 = (bf16[32,512]{1,0:T(8,128)(2,1)S(1)}, bf16[32,512]{1,0:T(8,128)(2,1)S(1)}, u32[]{:S(2)}, u32[]{:S(2)}) collective-permute-start(bf16[32,512]{1,0:T(8,128)(2,1)S(1)} %convert_element_type.47), channel_id=1, source_target_pairs={{0,8},{1,3},{2,10},{3,1},{4,12},{5,7},{6,14},{7,5},{8,0},{9,11},{1... | collective-permute-start | bytes 98312 | tf_op jit(solution)/shard_map/ppermute | solution.py:188
  20.1 0.3 %collective-permute-done.10 = bf16[32,512]{1,0:T(8,128)(2,1)S(1)} collective-permute-done((bf16[32,512]{1,0:T(8,128)(2,1)S(1)}, bf16[32,512]{1,0:T(8,128)(2,1)S(1)}, u32[]{:S(2)}, u32[]{:S(2)}) %collective-permute-start.10) | collective-permute-done | bytes 32800 | tf_op jit(solution)/shard_map/ppermute | solution.py:188
  20.4 1.6 %collective-permute-done.9 = bf16[32,512]{1,0:T(8,128)(2,1)S(1)} collective-permute-done((bf16[32,512]{1,0:T(8,128)(2,1)S(1)}, bf16[32,512]{1,0:T(8,128)(2,1)S(1)}, u32[]{:S(2)}, u32[]{:S(2)}) %collective-permute-start.9) | collective-permute-done | bytes 32800 | tf_op jit(solution)/shard_map/ppermute | solution.py:188
  22.0 0.4 %collective-permute-done.8 = bf16[32,512]{1,0:T(8,128)(2,1)S(1)} collective-permute-done((bf16[32,512]{1,0:T(8,128)(2,1)S(1)}, bf16[32,512]{1,0:T(8,128)(2,1)S(1)}, u32[]{:S(2)}, u32[]{:S(2)}) %collective-permute-start.8) | collective-permute-done | bytes 32800 | tf_op jit(solution)/shard_map/ppermute | solution.py:188
  22.5 0.1 collective-permute-start.11
  22.6 1.3 %collective-permute-done.11.received = f32[32,768]{1,0:T(8,128)S(1)} collective-permute-done((f32[32,768]{1,0:T(8,128)S(1)}, f32[32,768]{1,0:T(8,128)S(1)}, u32[]{:S(2)}, u32[]{:S(2)}) %collective-permute-start.11) | collective-permute-done | bytes 98336 | tf_op jit(solution)/shard_map/ppermute | solution.py:188
  23.9 0.0 copy-done.1
  23.9 0.8 %last.1 = f32[16,512]{1,0:T(8,128)} custom-call(s32[1]{0:T(128)} %bitcast.core, f32[32,512]{1,0:T(8,128)S(1)} %convert_add_fusion.incoming, f32[2,32,256]{2,1,0:T(8,128)S(1)} %get-tuple-element.11.near, f32[32,768]{1,0:T(8,128)S(1)} %collective-permute-done.11.received, bf16[2,512,256]{2,1,0:T(8,128)(2,1)S(1)} %bitcast.19, ...), custom_call_target="tpu_custom_call" | custom-call | tf_op jit(solution)/shard_map/last/pallas_call | solution.py:262
  (11 shorter events, 0.1 us)
Async XLA Ops:
  0.0 2.0 %copy-start = (bf16[1,4,2,64,512]{4,3,2,1,0:T(8,128)(2,1)S(1)}, bf16[1,4,2,64,512]{4,3,2,1,0:T(8,128)(2,1)}, u32[]{:S(2)}) copy-start(bf16[1,4,2,64,512]{4,3,2,1,0:T(8,128)(2,1)} %param.17) | copy-start | bytes 1572868
  1.5 12.8 %copy-start.2 = (bf16[225,2,512]{2,1,0:T(2,128)(2,1)S(1)}, bf16[225,2,512]{2,1,0:T(2,128)(2,1)}, u32[]{:S(2)}) copy-start(bf16[225,2,512]{2,1,0:T(2,128)(2,1)} %table.1) | copy-start | bytes 1382404
  1.5 1.5 %collective-permute-start.1 = (f32[40,768]{1,0:T(8,128)S(1)}, f32[40,768]{1,0:T(8,128)S(1)}, u32[]{:S(2)}, u32[]{:S(2)}) collective-permute-start(f32[40,768]{1,0:T(8,128)S(1)} %get-tuple-element.9), channel_id=1, source_target_pairs={{0,1},{1,0},{2,3},{3,2},{4,5},{5,4},{6,7},{7,6},{8,9},{9,8},{10,11... | collective-permute-start | bytes 368648 | tf_op jit(solution)/shard_map/ppermute | solution.py:188
  2.0 14.2 %collective-permute-start = (bf16[4,2,64,512]{3,2,1,0:T(8,128)(2,1)S(1)}, bf16[4,2,64,512]{3,2,1,0:T(8,128)(2,1)S(1)}, u32[]{:S(2)}, u32[]{:S(2)}) collective-permute-start(bf16[4,2,64,512]{3,2,1,0:T(8,128)(2,1)S(1)} %bitcast.17), channel_id=1, source_target_pairs={{0,1},{1,0},{2,3},{3,2},{4,5},{5,4},{6,7},{7,6},{8,9},{9,8},{10,11... | collective-permute-start | bytes 1572872 | tf_op jit(solution)/shard_map/ppermute | solution.py:188
  3.1 4.9 %collective-permute-start.2 = (bf16[32,640]{1,0:T(8,128)(2,1)S(1)}, bf16[32,640]{1,0:T(8,128)(2,1)S(1)}, u32[]{:S(2)}, u32[]{:S(2)}) collective-permute-start(bf16[32,640]{1,0:T(8,128)(2,1)S(1)} %get-tuple-element.16), channel_id=1, source_target_pairs={{0,8},{1,7},{2,10},{3,5},{4,12},{5,3},{6,14},{7,1},{8,0},{9,15},{1... | collective-permute-start | bytes 122888 | tf_op jit(solution)/shard_map/ppermute | solution.py:188
  6.0 4.0 %collective-permute-start.3 = (bf16[32,640]{1,0:T(8,128)(2,1)S(1)}, bf16[32,640]{1,0:T(8,128)(2,1)S(1)}, u32[]{:S(2)}, u32[]{:S(2)}) collective-permute-start(bf16[32,640]{1,0:T(8,128)(2,1)S(1)} %get-tuple-element.17), channel_id=1, source_target_pairs={{0,8},{1,5},{2,10},{3,7},{4,12},{5,1},{6,14},{7,3},{8,0},{9,13},{1... | collective-permute-start | bytes 122888 | tf_op jit(solution)/shard_map/ppermute | solution.py:188
  6.1 4.4 %collective-permute-start.4 = (bf16[32,640]{1,0:T(8,128)(2,1)S(1)}, bf16[32,640]{1,0:T(8,128)(2,1)S(1)}, u32[]{:S(2)}, u32[]{:S(2)}) collective-permute-start(bf16[32,640]{1,0:T(8,128)(2,1)S(1)} %get-tuple-element.18), channel_id=1, source_target_pairs={{0,8},{1,3},{2,10},{3,1},{4,12},{5,7},{6,14},{7,5},{8,0},{9,11},{1... | collective-permute-start | bytes 122888 | tf_op jit(solution)/shard_map/ppermute | solution.py:188
  10.4 3.8 %copy-start.3 = (s32[1,8]{1,0:T(1,128)S(1)}, s32[1,8]{1,0:T(1,128)}, u32[]{:S(2)}) copy-start(s32[1,8]{1,0:T(1,128)} %offsets_hbm.1) | copy-start | bytes 100
  10.4 3.8 %copy-start.4 = (s32[8]{0:T(128)S(1)}, s32[8]{0:T(128)}, u32[]{:S(2)}) copy-start(s32[8]{0:T(128)} %param.14) | copy-start | bytes 100
  10.5 5.2 %collective-permute-start.7 = (bf16[1,32,128]{2,1,0:T(8,128)(2,1)S(1)}, bf16[1,32,128]{2,1,0:T(8,128)(2,1)S(1)}, u32[]{:S(2)}, u32[]{:S(2)}) collective-permute-start(bf16[1,32,128]{2,1,0:T(8,128)(2,1)S(1)} %fusion.rest_0_), channel_id=1, source_target_pairs={{0,2},{1,25},{2,0},{3,27},{4,6},{5,29},{6,4},{7,31},{8,10},{9,17},... | collective-permute-start | bytes 24584 | tf_op jit(solution)/shard_map/ppermute | solution.py:188
  12.2 3.7 %collective-permute-start.6 = (bf16[1,32,128]{2,1,0:T(8,128)(2,1)S(1)}, bf16[1,32,128]{2,1,0:T(8,128)(2,1)S(1)}, u32[]{:S(2)}, u32[]{:S(2)}) collective-permute-start(bf16[1,32,128]{2,1,0:T(8,128)(2,1)S(1)} %fusion.rest_0_), channel_id=1, source_target_pairs={{0,2},{1,17},{2,0},{3,19},{4,6},{5,21},{6,4},{7,23},{8,10},{9,25},... | collective-permute-start | bytes 24584 | tf_op jit(solution)/shard_map/ppermute | solution.py:188
  12.5 3.7 %collective-permute-start.5 = (bf16[1,32,128]{2,1,0:T(8,128)(2,1)S(1)}, bf16[1,32,128]{2,1,0:T(8,128)(2,1)S(1)}, u32[]{:S(2)}, u32[]{:S(2)}) collective-permute-start(bf16[1,32,128]{2,1,0:T(8,128)(2,1)S(1)} %fusion.rest_0_), channel_id=1, source_target_pairs={{0,2},{1,9},{2,0},{3,11},{4,6},{5,13},{6,4},{7,15},{8,10},{9,1},{1... | collective-permute-start | bytes 24584 | tf_op jit(solution)/shard_map/ppermute | solution.py:188
  16.4 7.4 %copy-start.1 = (bf16[1,2,512,256]{3,2,1,0:T(8,128)(2,1)S(1)}, bf16[1,2,512,256]{3,2,1,0:T(8,128)(2,1)}, u32[]{:S(2)}) copy-start(bf16[1,2,512,256]{3,2,1,0:T(8,128)(2,1)} %param.16) | copy-start | bytes 1572868
  16.5 4.0 %collective-permute-start.10 = (bf16[32,512]{1,0:T(8,128)(2,1)S(1)}, bf16[32,512]{1,0:T(8,128)(2,1)S(1)}, u32[]{:S(2)}, u32[]{:S(2)}) collective-permute-start(bf16[32,512]{1,0:T(8,128)(2,1)S(1)} %convert_element_type.47), channel_id=1, source_target_pairs={{0,8},{1,7},{2,10},{3,5},{4,12},{5,3},{6,14},{7,1},{8,0},{9,15},{1... | collective-permute-start | bytes 98312 | tf_op jit(solution)/shard_map/ppermute | solution.py:188
  18.1 3.9 %collective-permute-start.9 = (bf16[32,512]{1,0:T(8,128)(2,1)S(1)}, bf16[32,512]{1,0:T(8,128)(2,1)S(1)}, u32[]{:S(2)}, u32[]{:S(2)}) collective-permute-start(bf16[32,512]{1,0:T(8,128)(2,1)S(1)} %convert_element_type.47), channel_id=1, source_target_pairs={{0,8},{1,5},{2,10},{3,7},{4,12},{5,1},{6,14},{7,3},{8,0},{9,13},{1... | collective-permute-start | bytes 98312 | tf_op jit(solution)/shard_map/ppermute | solution.py:188
  18.6 3.9 %collective-permute-start.8 = (bf16[32,512]{1,0:T(8,128)(2,1)S(1)}, bf16[32,512]{1,0:T(8,128)(2,1)S(1)}, u32[]{:S(2)}, u32[]{:S(2)}) collective-permute-start(bf16[32,512]{1,0:T(8,128)(2,1)S(1)} %convert_element_type.47), channel_id=1, source_target_pairs={{0,8},{1,3},{2,10},{3,1},{4,12},{5,7},{6,14},{7,5},{8,0},{9,11},{1... | collective-permute-start | bytes 98312 | tf_op jit(solution)/shard_map/ppermute | solution.py:188
  22.5 1.4 %collective-permute-start.11 = (f32[32,768]{1,0:T(8,128)S(1)}, f32[32,768]{1,0:T(8,128)S(1)}, u32[]{:S(2)}, u32[]{:S(2)}) collective-permute-start(f32[32,768]{1,0:T(8,128)S(1)} %pad_maximum_fusion), channel_id=1, source_target_pairs={{0,1},{1,0},{2,3},{3,2},{4,5},{5,4},{6,7},{7,6},{8,9},{9,8},{10,11... | collective-permute-start | bytes 294920 | tf_op jit(solution)/shard_map/ppermute | solution.py:188

commit v3 on v2

--- a/solution.py
+++ b/solution.py
@@ -36,10 +36,11 @@
 
 
 def first_kernel(
-    incident_hbm, offsets_hbm, t_hbm, up_hbm, scattered, message, incident, offsets, t_mats, up, sems
+    incident_hbm, offsets_hbm, t_hbm, up_hbm, exciting_hbm,
+    scattered, message, exciting, incident, offsets, t_mats, up, sems,
 ):
-    sources = (incident_hbm, t_hbm, offsets_hbm, up_hbm)
-    targets = (incident, t_mats, offsets, up)
+    sources = (incident_hbm, t_hbm, offsets_hbm, up_hbm, exciting_hbm)
+    targets = (incident, t_mats, offsets, up, exciting)
     copies = [
         pltpu.make_async_copy(source, target, sems.at[i])
         for i, (source, target) in enumerate(zip(sources, targets))
@@ -61,79 +62,76 @@
     own = crossed(own)
     copies[3].wait()
     message[:rows, :coefs] = dot(own, up[...].reshape(2 * modes, coefs))
-
-
-def first_call(incident, offsets, t_mats, up):
+    copies[4].wait()
+
+
+def first_call(incident, offsets, t_mats, up, exciting):
     rows, modes, coefs = 2 * incident.shape[0], up.shape[1], up.shape[2]
     return pl.pallas_call(
         first_kernel,
         out_shape=(
             shaped((rows, modes), BF16),
             shaped((rows + 8, coefs + modes), F32),
+            shaped(exciting.shape, F32),
         ),
-        in_specs=[HBM] * 4,
-        out_specs=(VMEM, VMEM),
+        in_specs=[HBM] * 5,
+        out_specs=(VMEM,) * 3,
         scratch_shapes=[
             pltpu.VMEM(incident.shape, BF16),
             pltpu.VMEM(offsets.shape, jnp.int32),
             pltpu.VMEM(t_mats.shape, BF16),
             pltpu.VMEM(up.shape, BF16),
-            pltpu.SemaphoreType.DMA((4,)),
+            pltpu.SemaphoreType.DMA((5,)),
         ],
         compiler_params=PARAMS,
         name="first",
-    )(*in_hbm(incident, offsets, t_mats, up))
-
-
-def near_kernel(places, members, core, chip, indices, exciting_hbm, table, *rest):
-    pieces, (near, exciting, sem) = rest[:-3], rest[-3:]
-    copy = pltpu.make_async_copy(exciting_hbm, exciting, sem)
-    copy.start()
-    _, rows, modes = near.shape
+    )(*in_hbm(incident, offsets, t_mats, up, exciting))
+
+
+def near_kernel(places, members, column, core, chip, indices, table, *rest):
+    pieces, near = rest[:-1], rest[-1]
+    rows, modes = near.shape
     half = modes // 2
 
     @pl.when(core[0] == 1)
     def _():
-        for column in range(2):
-            total = jnp.zeros((rows, 2 * modes), F32)
-            for other, piece, lane in places:
-                for member in range(2):
-                    if other == 0 and member == column:
-                        continue
-                    source = (chip[0] ^ other) * 2 + member
-                    slot = indices[2 * members + source]
-                    sequence = table[indices[column * members + slot]].astype(F32)
-                    mats = []
-                    for part in range(2):
-                        band = jnp.broadcast_to(sequence[part : part + 1], (half, 2 * modes))
-                        band = pltpu.roll(band, 0, 1, stride=1, stride_axis=0)
-                        band = band.astype(BF16)
-                        mats.append(
-                            jnp.concatenate(
-                                [band[:, modes:], band[:, half : half + modes]], axis=0
-                            )
-                        )
-                    start = lane + member * modes
-                    values = pieces[piece][:, start : start + modes]
-                    total += dot(values, jnp.concatenate(mats, axis=1))
-            top, low = total[: rows // 2], total[rows // 2 :]
-            near[column, : rows // 2, :] = top[:, :modes] - low[:, modes:]
-            near[column, rows // 2 :, :] = top[:, modes:] + low[:, :modes]
-
-    copy.wait()
-
-
-def group_kernel(places, group, own_maps, other_maps, *rest):
+        total = jnp.zeros((rows, 2 * modes), F32)
+        for other, piece, lane in places:
+            for member in range(2):
+                if other == 0 and member == column:
+                    continue
+                source = (chip[0] ^ other) * 2 + member
+                slot = indices[2 * members + source]
+                sequence = table[indices[column * members + slot]].astype(F32)
+                mats = []
+                for part in range(2):
+                    band = jnp.broadcast_to(sequence[part : part + 1], (half, 2 * modes))
+                    band = pltpu.roll(band, 0, 1, stride=1, stride_axis=0)
+                    band = band.astype(BF16)
+                    mats.append(
+                        jnp.concatenate([band[:, modes:], band[:, half : half + modes]], axis=0)
+                    )
+                start = lane + member * modes
+                values = pieces[piece][:, start : start + modes]
+                total += dot(values, jnp.concatenate(mats, axis=1))
+        top, low = total[: rows // 2], total[rows // 2 :]
+        near[: rows // 2, :] = top[:, :modes] - low[:, modes:]
+        near[rows // 2 :, :] = top[:, modes:] + low[:, :modes]
+
+
+def group_kernel(places, core, group, own_maps, other_maps, *rest):
     pieces, incoming = rest[:-1], rest[-1]
-    total = jnp.zeros(incoming.shape, F32)
-    for other, piece, index in places:
-        source = group[0] ^ other
-        mats = jnp.concatenate(
-            [other_maps[source, 0], own_maps[source, 0], other_maps[source, 1], own_maps[source, 1]],
-            axis=0,
-        )
-        total += dot(crossed(pieces[piece][index]), mats)
-    incoming[...] = total
+
+    @pl.when(core[0] == 1)
+    def _():
+        total = jnp.zeros(incoming.shape, F32)
+        for other, piece, index in places:
+            source = group[0] ^ other
+            mats = [
+                maps[source, part] for part in range(2) for maps in (other_maps, own_maps)
+            ]
+            total += dot(crossed(pieces[piece][index]), jnp.concatenate(mats, axis=0))
+        incoming[...] = total
 
 
 def last_kernel(core, incoming, near, received, down, exciting, updated):
@@ -151,7 +149,7 @@
 
     @pl.when(core[0] == 1)
     def _():
-        finish(incoming[...], near[1])
+        finish(incoming[...], near[...])
 
 
 def digits(count):
@@ -188,7 +186,9 @@
         return lax.ppermute(values, AXES, pairs)
 
     core_at, chip_at, group_at = (x.astype(jnp.int32).reshape(1) for x in (core, chip, group))
-    scattered, message = first_call(incident[0], offsets, t_matrices[0], up_maps[0])
+    scattered, message, exciting_early = first_call(
+        incident[0], offsets, t_matrices[0], up_maps[0], exciting[0]
+    )
     rows = scattered.shape[0]
     received = exchange(message, 1, 1)
     other_maps = exchange(group_maps[0], 1, 1)
@@ -200,7 +200,7 @@
     )
     pieces = [jnp.concatenate([received[:rows, coefs:].astype(BF16), scattered], axis=1)]
     places = [(0, 0, 0)]
-    aside = bodies if groups > 1 else 2
+    aside = [bodies << bit for bit in range(groups.bit_length() - 1)] or [2]
     for steps in digits(chips):
         width = expansion.shape[1] // (len(steps) + 1)
         unit = min(steps)
@@ -214,7 +214,10 @@
             jnp.concatenate(gathered + [part(own ^ (step // unit)).astype(BF16)], axis=1)
             for step in steps
         ]
-        arrived = [exchange(m, aside, 2 * step) for m, step in zip(messages, steps)]
+        arrived = [
+            exchange(message, aside[i % len(aside)], 2 * step)
+            for i, (message, step) in enumerate(zip(messages, steps))
+        ]
         held = len(places)
         expansion = part(own)
         for step, piece in zip(steps, arrived):
@@ -225,15 +228,19 @@
             ]
             pieces.append(piece)
 
-    near, exciting_near = pl.pallas_call(
-        functools.partial(near_kernel, tuple(places), members),
-        out_shape=(shaped((2, rows, modes), F32), shaped(exciting.shape[1:], F32)),
-        in_specs=[SMEM] * 3 + [HBM, VMEM] + [VMEM] * len(pieces),
-        out_specs=(VMEM, VMEM),
-        scratch_shapes=[pltpu.SemaphoreType.DMA],
-        compiler_params=PARAMS,
-        name="near",
-    )(core_at, chip_at, indices, *in_hbm(exciting[0]), hankel_rows, *pieces)
+    def near_call(column, *pieces):
+        size = len(pieces) * rows * modes * modes
+        return pl.pallas_call(
+            functools.partial(near_kernel, tuple(places), members, column),
+            out_shape=shaped((rows, modes), F32),
+            in_specs=[SMEM] * 3 + [VMEM] * (1 + len(pieces)),
+            out_specs=VMEM,
+            compiler_params=PARAMS,
+            cost_estimate=pl.CostEstimate(flops=8 * size, bytes_accessed=size, transcendentals=0),
+            name="near",
+        )(core_at, chip_at, indices, hankel_rows, *pieces)
+
+    near = [near_call(column, *pieces) for column in range(2)]
 
     blocks = [expansion.astype(BF16)[None]]
     group_places = [(0, 0, 0)]
@@ -247,15 +254,19 @@
     incoming = pl.pallas_call(
         functools.partial(group_kernel, tuple(group_places[1:])),
         out_shape=shaped((rows, coefs), F32),
-        in_specs=[SMEM] + [VMEM] * (2 + len(blocks)),
+        in_specs=[SMEM] * 2 + [VMEM] * (2 + len(blocks)),
         out_specs=VMEM,
         compiler_params=PARAMS,
         name="group",
-    )(group_at, group_maps[0], other_maps, *blocks)
+    )(core_at, group_at, group_maps[0], other_maps, *blocks)
 
     for steps in digits(chips):
         message = incoming.astype(BF16)
-        for piece in [exchange(message, aside, 2 * step) for step in reversed(steps)]:
+        arrived = [
+            exchange(message, aside[i % len(aside)], 2 * step)
+            for i, step in enumerate(reversed(steps))
+        ]
+        for piece in arrived:
             incoming += piece.astype(F32)
 
     received = exchange(jnp.concatenate([incoming, near[0]], axis=1), 1, 1)
@@ -266,7 +277,7 @@
         out_specs=VMEM,
         compiler_params=PARAMS,
         name="last",
-    )(core_at, incoming, near, received, down_maps[0], exciting_near)[None]
+    )(core_at, incoming, near[1], received, down_maps[0], exciting_early)[None]
 
 
 def solution(mesh):

time: 24.9 us -> 24.6 us (0.988)
  waiting for transfers between devices: 7.45 us -> 8.22 us
  starting transfers between devices: 13.1 us -> 12.5 us
  Pallas kernels: 3.81 us -> 3.36 us
    ppermute x12, waiting for transfers between devices: 7.45 us -> 8.22 us  [exchange(): return lax.ppermute(values, AXES, pairs)]
    ppermute x12, starting transfers between devices: 13.1 us -> 12.5 us  [exchange(): return lax.ppermute(values, AXES, pairs)]
    pallas_call x1 -> x2, Pallas kernels: 1.31 us -> 1.09 us  [near_call(): pl.pallas_call(functools.partial(near_kernel, tuple(places), members, col...]
  transfers between devices with their start and end apart: 12 -> 12, of which waited for: 9 -> 9; matrix products, arithmetic and copies ran while one was open for 1% -> 1% of each run, Pallas kernels for 5% -> 4%
where the time goes in v3:
time: 24.6 us; the launch traced here: 24.4 us
  starting transfers between devices  12.5 us (51%)
  waiting for transfers between devices  8.22 us (33%)
  Pallas kernels  3.36 us (14%)
    ppermute x12, starting transfers between devices, exchange(): return lax.ppermute(values, AXES, pairs)  12.5 us
    ppermute x12, waiting for transfers between devices, exchange(): return lax.ppermute(values, AXES, pairs)  8.22 us
    pallas_call x1, Pallas kernels, first_call(): pl.pallas_call(first_kernel, out_shape=(shaped((rows, modes), BF16), shap...  1.45 us
    pallas_call x2, Pallas kernels, near_call(): pl.pallas_call(functools.partial(near_kernel, tuple(places), members, col...  1.09 us
    pallas_call x1, Pallas kernels, local(): pl.pallas_call(last_kernel, out_shape=shaped(exciting.shape[1:], F32), in...  0.82 us
  transfers between devices with their start and end apart: 12, of which 9 were waited for; matrix products, arithmetic and copies ran while one was open for 1% of the time, Pallas kernels for 4%

profile of v3, /device:TPU:0, one launch (start us, length us, event | category | flops | bytes accessed | tf_op | source)
XLA Modules:
  0.0 24.4 jit_solution(12136562616857775570)
XLA Ops:
  0.0 0.0 copy-start.2
  0.0 1.5 %first.1 = (bf16[32,256]{1,0:T(8,128)(2,1)S(1)}, f32[40,768]{1,0:T(8,128)S(1)}, f32[16,512]{1,0:T(8,128)S(1)}) custom-call(bf16[16,512]{1,0:T(8,128)(2,1)} %bitcast.21, s32[1,8]{1,0:T(1,128)} %offsets_hbm.1, bf16[2,256,256]{2,1,0:T(8,128)(2,1)} %bitcast.19, bf16[2,256,512]{2,1,0:T(8,128)(2,1)} %bitcast.18, f32[16,512]{1,0:T(8,128)} %bitcast.20), custom_call_target="tpu_custom_call" | custom-call | tf_op jit(solution)/shard_map/first/pallas_call | solution.py:70
  1.5 0.6 %collective-permute-start.1 = (f32[40,768]{1,0:T(8,128)S(1)}, f32[40,768]{1,0:T(8,128)S(1)}, u32[]{:S(2)}, u32[]{:S(2)}) collective-permute-start(f32[40,768]{1,0:T(8,128)S(1)} %get-tuple-element.8), channel_id=1, source_target_pairs={{0,1},{1,0},{2,3},{3,2},{4,5},{5,4},{6,7},{7,6},{8,9},{9,8},{10,11... | collective-permute-start | bytes 368648 | tf_op jit(solution)/shard_map/ppermute | solution.py:186
  2.0 0.0 copy-done.2
  2.0 0.1 collective-permute-start
  2.1 0.9 %collective-permute-done.1 = f32[40,768]{1,0:T(8,128)S(1)} collective-permute-done((f32[40,768]{1,0:T(8,128)S(1)}, f32[40,768]{1,0:T(8,128)S(1)}, u32[]{:S(2)}, u32[]{:S(2)}) %collective-permute-start.1) | collective-permute-done | bytes 122912 | tf_op jit(solution)/shard_map/ppermute | solution.py:186
  3.1 2.9 %collective-permute-start.2 = (bf16[32,640]{1,0:T(8,128)(2,1)S(1)}, bf16[32,640]{1,0:T(8,128)(2,1)S(1)}, u32[]{:S(2)}, u32[]{:S(2)}) collective-permute-start(bf16[32,640]{1,0:T(8,128)(2,1)S(1)} %get-tuple-element.14), channel_id=1, source_target_pairs={{0,8},{1,7},{2,10},{3,5},{4,12},{5,3},{6,14},{7,1},{8,0},{9,15},{1... | collective-permute-start | bytes 122888 | tf_op jit(solution)/shard_map/ppermute | solution.py:186
  6.0 1.5 %collective-permute-start.3 = (bf16[32,640]{1,0:T(8,128)(2,1)S(1)}, bf16[32,640]{1,0:T(8,128)(2,1)S(1)}, u32[]{:S(2)}, u32[]{:S(2)}) collective-permute-start(bf16[32,640]{1,0:T(8,128)(2,1)S(1)} %get-tuple-element.15), channel_id=1, source_target_pairs={{0,16},{1,5},{2,18},{3,7},{4,20},{5,1},{6,22},{7,3},{8,24},{9,13},... | collective-permute-start | bytes 122888 | tf_op jit(solution)/shard_map/ppermute | solution.py:186
  7.5 0.5 %collective-permute-start.4 = (bf16[32,640]{1,0:T(8,128)(2,1)S(1)}, bf16[32,640]{1,0:T(8,128)(2,1)S(1)}, u32[]{:S(2)}, u32[]{:S(2)}) collective-permute-start(bf16[32,640]{1,0:T(8,128)(2,1)S(1)} %get-tuple-element.16), channel_id=1, source_target_pairs={{0,8},{1,3},{2,10},{3,1},{4,12},{5,7},{6,14},{7,5},{8,0},{9,11},{1... | collective-permute-start | bytes 122888 | tf_op jit(solution)/shard_map/ppermute | solution.py:186
  8.0 0.0 collective-permute-done.2.rest_1_
  8.0 1.9 %collective-permute-done.3.rest_2_ = bf16[32,640]{1,0:T(8,128)(2,1)S(1)} collective-permute-done((bf16[32,640]{1,0:T(8,128)(2,1)S(1)}, bf16[32,640]{1,0:T(8,128)(2,1)S(1)}, u32[]{:S(2)}, u32[]{:S(2)}) %collective-permute-start.3) | collective-permute-done | bytes 40992 | tf_op jit(solution)/shard_map/ppermute | solution.py:186
  10.0 1.5 %collective-permute-done.4.rest_3_ = bf16[32,640]{1,0:T(8,128)(2,1)S(1)} collective-permute-done((bf16[32,640]{1,0:T(8,128)(2,1)S(1)}, bf16[32,640]{1,0:T(8,128)(2,1)S(1)}, u32[]{:S(2)}, u32[]{:S(2)}) %collective-permute-start.4) | collective-permute-done | bytes 40992 | tf_op jit(solution)/shard_map/ppermute | solution.py:186
  11.5 1.6 %collective-permute-start.7 = (bf16[1,32,128]{2,1,0:T(8,128)(2,1)S(1)}, bf16[1,32,128]{2,1,0:T(8,128)(2,1)S(1)}, u32[]{:S(2)}, u32[]{:S(2)}) collective-permute-start(bf16[1,32,128]{2,1,0:T(8,128)(2,1)S(1)} %fusion.rest_0_), channel_id=1, source_target_pairs={{0,2},{1,25},{2,0},{3,27},{4,6},{5,29},{6,4},{7,31},{8,10},{9,17},... | collective-permute-start | bytes 24584 | tf_op jit(solution)/shard_map/ppermute | solution.py:186
  13.2 0.5 %collective-permute-start.6 = (bf16[1,32,128]{2,1,0:T(8,128)(2,1)S(1)}, bf16[1,32,128]{2,1,0:T(8,128)(2,1)S(1)}, u32[]{:S(2)}, u32[]{:S(2)}) collective-permute-start(bf16[1,32,128]{2,1,0:T(8,128)(2,1)S(1)} %fusion.rest_0_), channel_id=1, source_target_pairs={{0,2},{1,17},{2,0},{3,19},{4,6},{5,21},{6,4},{7,23},{8,10},{9,25},... | collective-permute-start | bytes 24584 | tf_op jit(solution)/shard_map/ppermute | solution.py:186
  13.6 1.6 %collective-permute-start.5 = (bf16[1,32,128]{2,1,0:T(8,128)(2,1)S(1)}, bf16[1,32,128]{2,1,0:T(8,128)(2,1)S(1)}, u32[]{:S(2)}, u32[]{:S(2)}) collective-permute-start(bf16[1,32,128]{2,1,0:T(8,128)(2,1)S(1)} %fusion.rest_0_), channel_id=1, source_target_pairs={{0,2},{1,9},{2,0},{3,11},{4,6},{5,13},{6,4},{7,15},{8,10},{9,1},{1... | collective-permute-start | bytes 24584 | tf_op jit(solution)/shard_map/ppermute | solution.py:186
  15.2 0.0 collective-permute-done.7.rest_3_
  15.2 1.6 %collective-permute-done.6.rest_2_ = bf16[1,32,128]{2,1,0:T(8,128)(2,1)S(1)} collective-permute-done((bf16[1,32,128]{2,1,0:T(8,128)(2,1)S(1)}, bf16[1,32,128]{2,1,0:T(8,128)(2,1)S(1)}, u32[]{:S(2)}, u32[]{:S(2)}) %collective-permute-start.6) | collective-permute-done | bytes 8224 | tf_op jit(solution)/shard_map/ppermute | solution.py:186
  16.8 0.5 %collective-permute-done.5.rest_1_ = bf16[1,32,128]{2,1,0:T(8,128)(2,1)S(1)} collective-permute-done((bf16[1,32,128]{2,1,0:T(8,128)(2,1)S(1)}, bf16[1,32,128]{2,1,0:T(8,128)(2,1)S(1)}, u32[]{:S(2)}, u32[]{:S(2)}) %collective-permute-start.5) | collective-permute-done | bytes 8224 | tf_op jit(solution)/shard_map/ppermute | solution.py:186
  17.3 0.0 collective-permute-done.other_maps
  17.3 0.0 copy-start
  17.3 0.0 copy-start.3
  17.3 0.0 copy-start.4
  17.3 0.6 %collective-permute-start.10 = (bf16[32,512]{1,0:T(8,128)(2,1)S(1)}, bf16[32,512]{1,0:T(8,128)(2,1)S(1)}, u32[]{:S(2)}, u32[]{:S(2)}) collective-permute-start(bf16[32,512]{1,0:T(8,128)(2,1)S(1)} %convert_element_type.47), channel_id=1, source_target_pairs={{0,8},{1,7},{2,10},{3,5},{4,12},{5,3},{6,14},{7,1},{8,0},{9,15},{1... | collective-permute-start | bytes 98312 | tf_op jit(solution)/shard_map/ppermute | solution.py:186
  17.9 0.1 collective-permute-start.9
  18.0 1.9 %collective-permute-start.8 = (bf16[32,512]{1,0:T(8,128)(2,1)S(1)}, bf16[32,512]{1,0:T(8,128)(2,1)S(1)}, u32[]{:S(2)}, u32[]{:S(2)}) collective-permute-start(bf16[32,512]{1,0:T(8,128)(2,1)S(1)} %convert_element_type.47), channel_id=1, source_target_pairs={{0,8},{1,3},{2,10},{3,1},{4,12},{5,7},{6,14},{7,5},{8,0},{9,11},{1... | collective-permute-start | bytes 98312 | tf_op jit(solution)/shard_map/ppermute | solution.py:186
  19.9 0.0 copy-done.3
  19.9 0.0 copy-done.4
  19.9 0.1 pad_add_fusion.indices
  20.0 0.0 copy-done
  20.0 0.5 %near.3 = f32[32,256]{1,0:T(8,128)S(1)} custom-call(s32[1]{0:T(128)} %bitcast.core, s32[1]{0:T(128)} %bitcast.8.chip, s32[24]{0:T(128)S(1)} %pad_add_fusion.indices, bf16[225,2,512]{2,1,0:T(2,128)(2,1)S(1)} %copy-done, bf16[32,512]{1,0:T(8,128)(2,1)S(1)} %pad_maximum_fusion.5.rest_0_, bf16[32,640]{1,0:T(8,128)(2,1)S(1)} %collective-permute-done.2.rest_1_, ...), custom_call_target="tpu_custom_call" | custom-call | flops 67108864 | bytes 8388608 | tf_op jit(solution)/shard_map/near/pallas_call | solution.py:233
  20.5 0.0 copy-start.1
  20.5 0.7 %collective-permute-done.10 = bf16[32,512]{1,0:T(8,128)(2,1)S(1)} collective-permute-done((bf16[32,512]{1,0:T(8,128)(2,1)S(1)}, bf16[32,512]{1,0:T(8,128)(2,1)S(1)}, u32[]{:S(2)}, u32[]{:S(2)}) %collective-permute-start.10) | collective-permute-done | bytes 32800 | tf_op jit(solution)/shard_map/ppermute | solution.py:186
  21.3 0.5 %collective-permute-done.9 = bf16[32,512]{1,0:T(8,128)(2,1)S(1)} collective-permute-done((bf16[32,512]{1,0:T(8,128)(2,1)S(1)}, bf16[32,512]{1,0:T(8,128)(2,1)S(1)}, u32[]{:S(2)}, u32[]{:S(2)}) %collective-permute-start.9) | collective-permute-done | bytes 32800 | tf_op jit(solution)/shard_map/ppermute | solution.py:186
  21.8 0.1 collective-permute-done.8
  22.0 0.7 %collective-permute-start.11 = (f32[32,768]{1,0:T(8,128)S(1)}, f32[32,768]{1,0:T(8,128)S(1)}, u32[]{:S(2)}, u32[]{:S(2)}) collective-permute-start(f32[32,768]{1,0:T(8,128)S(1)} %pad_maximum_fusion), channel_id=1, source_target_pairs={{0,1},{1,0},{2,3},{3,2},{4,5},{5,4},{6,7},{7,6},{8,9},{9,8},{10,11... | collective-permute-start | bytes 294920 | tf_op jit(solution)/shard_map/ppermute | solution.py:186
  22.6 0.5 %near.2 = f32[32,256]{1,0:T(8,128)S(1)} custom-call(s32[1]{0:T(128)} %bitcast.core, s32[1]{0:T(128)} %bitcast.8.chip, s32[24]{0:T(128)S(1)} %pad_add_fusion.indices, bf16[225,2,512]{2,1,0:T(2,128)(2,1)S(1)} %copy-done, bf16[32,512]{1,0:T(8,128)(2,1)S(1)} %pad_maximum_fusion.5.rest_0_, bf16[32,640]{1,0:T(8,128)(2,1)S(1)} %collective-permute-done.2.rest_1_, ...), custom_call_target="tpu_custom_call" | custom-call | flops 67108864 | bytes 8388608 | tf_op jit(solution)/shard_map/near/pallas_call | solution.py:233
  23.2 0.4 %collective-permute-done.11.received = f32[32,768]{1,0:T(8,128)S(1)} collective-permute-done((f32[32,768]{1,0:T(8,128)S(1)}, f32[32,768]{1,0:T(8,128)S(1)}, u32[]{:S(2)}, u32[]{:S(2)}) %collective-permute-start.11) | collective-permute-done | bytes 98336 | tf_op jit(solution)/shard_map/ppermute | solution.py:186
  23.6 0.0 copy-done.1
  23.6 0.8 %last.1 = f32[16,512]{1,0:T(8,128)} custom-call(s32[1]{0:T(128)} %bitcast.core, f32[32,512]{1,0:T(8,128)S(1)} %convert_add_fusion.incoming, f32[32,256]{1,0:T(8,128)S(1)} %near.2, f32[32,768]{1,0:T(8,128)S(1)} %collective-permute-done.11.received, bf16[2,512,256]{2,1,0:T(8,128)(2,1)S(1)} %bitcast.15, f32[16,512]{1,0:T(8,128)S(1)} %get-tuple-element.10.exciting), custom_call_target="tpu_custom_call" | custom-call | tf_op jit(solution)/shard_map/last/pallas_call | solution.py:273
  (11 shorter events, 0.1 us)
Async XLA Ops:
  0.0 2.0 %copy-start.2 = (bf16[1,4,2,64,512]{4,3,2,1,0:T(8,128)(2,1)S(1)}, bf16[1,4,2,64,512]{4,3,2,1,0:T(8,128)(2,1)}, u32[]{:S(2)}) copy-start(bf16[1,4,2,64,512]{4,3,2,1,0:T(8,128)(2,1)} %param.17) | copy-start | bytes 1572868
  1.5 1.5 %collective-permute-start.1 = (f32[40,768]{1,0:T(8,128)S(1)}, f32[40,768]{1,0:T(8,128)S(1)}, u32[]{:S(2)}, u32[]{:S(2)}) collective-permute-start(f32[40,768]{1,0:T(8,128)S(1)} %get-tuple-element.8), channel_id=1, source_target_pairs={{0,1},{1,0},{2,3},{3,2},{4,5},{5,4},{6,7},{7,6},{8,9},{9,8},{10,11... | collective-permute-start | bytes 368648 | tf_op jit(solution)/shard_map/ppermute | solution.py:186
  2.0 15.2 %collective-permute-start = (bf16[4,2,64,512]{3,2,1,0:T(8,128)(2,1)S(1)}, bf16[4,2,64,512]{3,2,1,0:T(8,128)(2,1)S(1)}, u32[]{:S(2)}, u32[]{:S(2)}) collective-permute-start(bf16[4,2,64,512]{3,2,1,0:T(8,128)(2,1)S(1)} %bitcast.16), channel_id=1, source_target_pairs={{0,1},{1,0},{2,3},{3,2},{4,5},{5,4},{6,7},{7,6},{8,9},{9,8},{10,11... | collective-permute-start | bytes 1572872 | tf_op jit(solution)/shard_map/ppermute | solution.py:186
  3.1 5.0 %collective-permute-start.2 = (bf16[32,640]{1,0:T(8,128)(2,1)S(1)}, bf16[32,640]{1,0:T(8,128)(2,1)S(1)}, u32[]{:S(2)}, u32[]{:S(2)}) collective-permute-start(bf16[32,640]{1,0:T(8,128)(2,1)S(1)} %get-tuple-element.14), channel_id=1, source_target_pairs={{0,8},{1,7},{2,10},{3,5},{4,12},{5,3},{6,14},{7,1},{8,0},{9,15},{1... | collective-permute-start | bytes 122888 | tf_op jit(solution)/shard_map/ppermute | solution.py:186
  6.0 4.0 %collective-permute-start.3 = (bf16[32,640]{1,0:T(8,128)(2,1)S(1)}, bf16[32,640]{1,0:T(8,128)(2,1)S(1)}, u32[]{:S(2)}, u32[]{:S(2)}) collective-permute-start(bf16[32,640]{1,0:T(8,128)(2,1)S(1)} %get-tuple-element.15), channel_id=1, source_target_pairs={{0,16},{1,5},{2,18},{3,7},{4,20},{5,1},{6,22},{7,3},{8,24},{9,13},... | collective-permute-start | bytes 122888 | tf_op jit(solution)/shard_map/ppermute | solution.py:186
  7.5 4.0 %collective-permute-start.4 = (bf16[32,640]{1,0:T(8,128)(2,1)S(1)}, bf16[32,640]{1,0:T(8,128)(2,1)S(1)}, u32[]{:S(2)}, u32[]{:S(2)}) collective-permute-start(bf16[32,640]{1,0:T(8,128)(2,1)S(1)} %get-tuple-element.16), channel_id=1, source_target_pairs={{0,8},{1,3},{2,10},{3,1},{4,12},{5,7},{6,14},{7,5},{8,0},{9,11},{1... | collective-permute-start | bytes 122888 | tf_op jit(solution)/shard_map/ppermute | solution.py:186
  11.5 3.7 %collective-permute-start.7 = (bf16[1,32,128]{2,1,0:T(8,128)(2,1)S(1)}, bf16[1,32,128]{2,1,0:T(8,128)(2,1)S(1)}, u32[]{:S(2)}, u32[]{:S(2)}) collective-permute-start(bf16[1,32,128]{2,1,0:T(8,128)(2,1)S(1)} %fusion.rest_0_), channel_id=1, source_target_pairs={{0,2},{1,25},{2,0},{3,27},{4,6},{5,29},{6,4},{7,31},{8,10},{9,17},... | collective-permute-start | bytes 24584 | tf_op jit(solution)/shard_map/ppermute | solution.py:186
  13.2 3.7 %collective-permute-start.6 = (bf16[1,32,128]{2,1,0:T(8,128)(2,1)S(1)}, bf16[1,32,128]{2,1,0:T(8,128)(2,1)S(1)}, u32[]{:S(2)}, u32[]{:S(2)}) collective-permute-start(bf16[1,32,128]{2,1,0:T(8,128)(2,1)S(1)} %fusion.rest_0_), channel_id=1, source_target_pairs={{0,2},{1,17},{2,0},{3,19},{4,6},{5,21},{6,4},{7,23},{8,10},{9,25},... | collective-permute-start | bytes 24584 | tf_op jit(solution)/shard_map/ppermute | solution.py:186
  13.6 3.7 %collective-permute-start.5 = (bf16[1,32,128]{2,1,0:T(8,128)(2,1)S(1)}, bf16[1,32,128]{2,1,0:T(8,128)(2,1)S(1)}, u32[]{:S(2)}, u32[]{:S(2)}) collective-permute-start(bf16[1,32,128]{2,1,0:T(8,128)(2,1)S(1)} %fusion.rest_0_), channel_id=1, source_target_pairs={{0,2},{1,9},{2,0},{3,11},{4,6},{5,13},{6,4},{7,15},{8,10},{9,1},{1... | collective-permute-start | bytes 24584 | tf_op jit(solution)/shard_map/ppermute | solution.py:186
  17.3 2.7 %copy-start = (bf16[225,2,512]{2,1,0:T(2,128)(2,1)S(1)}, bf16[225,2,512]{2,1,0:T(2,128)(2,1)}, u32[]{:S(2)}) copy-start(bf16[225,2,512]{2,1,0:T(2,128)(2,1)} %table.3) | copy-start | bytes 1382404
  17.3 2.6 %copy-start.3 = (s32[1,8]{1,0:T(1,128)S(1)}, s32[1,8]{1,0:T(1,128)}, u32[]{:S(2)}) copy-start(s32[1,8]{1,0:T(1,128)} %offsets_hbm.1) | copy-start | bytes 100
  17.3 2.6 %copy-start.4 = (s32[8]{0:T(128)S(1)}, s32[8]{0:T(128)}, u32[]{:S(2)}) copy-start(s32[8]{0:T(128)} %param.14) | copy-start | bytes 100
  17.3 4.0 %collective-permute-start.10 = (bf16[32,512]{1,0:T(8,128)(2,1)S(1)}, bf16[32,512]{1,0:T(8,128)(2,1)S(1)}, u32[]{:S(2)}, u32[]{:S(2)}) collective-permute-start(bf16[32,512]{1,0:T(8,128)(2,1)S(1)} %convert_element_type.47), channel_id=1, source_target_pairs={{0,8},{1,7},{2,10},{3,5},{4,12},{5,3},{6,14},{7,1},{8,0},{9,15},{1... | collective-permute-start | bytes 98312 | tf_op jit(solution)/shard_map/ppermute | solution.py:186
  17.9 3.9 %collective-permute-start.9 = (bf16[32,512]{1,0:T(8,128)(2,1)S(1)}, bf16[32,512]{1,0:T(8,128)(2,1)S(1)}, u32[]{:S(2)}, u32[]{:S(2)}) collective-permute-start(bf16[32,512]{1,0:T(8,128)(2,1)S(1)} %convert_element_type.47), channel_id=1, source_target_pairs={{0,16},{1,5},{2,18},{3,7},{4,20},{5,1},{6,22},{7,3},{8,24},{9,13},... | collective-permute-start | bytes 98312 | tf_op jit(solution)/shard_map/ppermute | solution.py:186
  18.0 3.9 %collective-permute-start.8 = (bf16[32,512]{1,0:T(8,128)(2,1)S(1)}, bf16[32,512]{1,0:T(8,128)(2,1)S(1)}, u32[]{:S(2)}, u32[]{:S(2)}) collective-permute-start(bf16[32,512]{1,0:T(8,128)(2,1)S(1)} %convert_element_type.47), channel_id=1, source_target_pairs={{0,8},{1,3},{2,10},{3,1},{4,12},{5,7},{6,14},{7,5},{8,0},{9,11},{1... | collective-permute-start | bytes 98312 | tf_op jit(solution)/shard_map/ppermute | solution.py:186
  20.5 3.1 %copy-start.1 = (bf16[1,2,512,256]{3,2,1,0:T(8,128)(2,1)S(1)}, bf16[1,2,512,256]{3,2,1,0:T(8,128)(2,1)}, u32[]{:S(2)}) copy-start(bf16[1,2,512,256]{3,2,1,0:T(8,128)(2,1)} %param.16) | copy-start | bytes 1572868
  22.0 1.6 %collective-permute-start.11 = (f32[32,768]{1,0:T(8,128)S(1)}, f32[32,768]{1,0:T(8,128)S(1)}, u32[]{:S(2)}, u32[]{:S(2)}) collective-permute-start(f32[32,768]{1,0:T(8,128)S(1)} %pad_maximum_fusion), channel_id=1, source_target_pairs={{0,1},{1,0},{2,3},{3,2},{4,5},{5,4},{6,7},{7,6},{8,9},{9,8},{10,11... | collective-permute-start | bytes 294920 | tf_op jit(solution)/shard_map/ppermute | solution.py:186
